TPU v7x, 32 devices: a whole 2x2x4 slice. The times are simulated.
32 devices in a mesh: dp: 8 (over z, y), expert: 4 (over x, core).
Axes of the slice: x: 2, y: 2, z: 4, core: 2. Of those that a mesh axis runs over, the one named last changes fastest.
Arguments:
- tokens: bfloat16 [4096, 1024], P(('dp', 'expert')), may hold values from -6 to 6
- route_ids: int32 [4096, 1], P(('dp', 'expert')), may hold values from 0 to 3; in each aligned block of 128 rows (0 to 127, 128 to 255, ...) at most 48 rows name the same one
- route_weight: float32 [4096, 1], P(('dp', 'expert')), may hold values from 0.02 to 0.5
- w_gate_up: bfloat16 [4, 1024, 768], P('expert'), may hold values from -0.1875 to 0.1875
- w_down: bfloat16 [4, 384, 1024], P('expert'), may hold values from -0.3125 to 0.3125
- out_grad: bfloat16 [4096, 1024], P(('dp', 'expert')), may hold values from -6 to 6
Outputs:
- mixed: bfloat16 [4096, 1024], P(('dp', 'expert'))
- token_grad: bfloat16 [4096, 1024], P(('dp', 'expert'))
- route_weight_grad: float32 [4096, 1], P(('dp', 'expert'))
- weight_grad: float32 [4, 1024, 1152], P('expert', 'dp')
Inputs may be any that keep to these rules, and one draw needn't show every extreme that they name: `route_ids`: among the 128 rows of one device (aligned blocks), no expert is named by more than 48 rows, a bound that some block reaches; a row names 1 different experts.
All inputs are finite; a program needn't handle non-finite values.
Results may differ from a plain program's by a relative error of at most 0.0057.
Values may be sent and summed in bfloat16 or wider, within the bound.
No kernel may reach another device: no remote copies, remote signals or barrier semaphores. Data moves between devices by JAX's collectives and lax.ppermute only.
A program may use at most 64 MiB of HBM per device.

v0:
```python
import functools

import jax
import jax.numpy as jnp
from jax import lax
from jax.experimental import pallas as pl
from jax.experimental.pallas import tpu as pltpu
from jax.sharding import PartitionSpec as P


BF = jnp.bfloat16
F32 = jnp.float32
VMEM = pl.BlockSpec(memory_space=pltpu.VMEM)
FAR = pl.BlockSpec(memory_space=pltpu.HBM)


def dot(left, right, left_axis, right_axis):
    return lax.dot_general(
        left, right, (((left_axis,), (right_axis,)), ((), ())), preferred_element_type=F32
    )


def call(body, outs, args, scratch=(), flops=0, far_ins=(), far_outs=(), aliases=None):
    size = sum(a.size * a.dtype.itemsize for a in args)
    size += sum(o.size * o.dtype.itemsize for o in outs)
    args = [pltpu.with_memory_space_constraint(a, pltpu.HBM) if k in far_ins else a for k, a in enumerate(args)]
    return pl.pallas_call(
        body,
        out_shape=list(outs),
        in_specs=[FAR if k in far_ins else VMEM for k in range(len(args))],
        out_specs=[FAR if k in far_outs else VMEM for k in range(len(outs))],
        scratch_shapes=list(scratch),
        input_output_aliases=aliases or {},
        cost_estimate=pl.CostEstimate(flops=flops, bytes_accessed=size, transcendentals=0),
        compiler_params=pltpu.CompilerParams(vmem_limit_bytes=24 << 20),
    )(*args)


def shape(dims, dtype):
    return jax.ShapeDtypeStruct(dims, dtype)


def row_to_column(row):
    count = row.shape[1]
    at = lax.broadcasted_iota(jnp.int32, (count, count), 0)
    to = lax.broadcasted_iota(jnp.int32, (count, count), 1)
    return jnp.sum(jnp.where(at == to, jnp.broadcast_to(row, (count, count)), 0.0), axis=1, keepdims=True)


def column_to_row(column):
    count = column.shape[0]
    at = lax.broadcasted_iota(jnp.int32, (count, count), 0)
    to = lax.broadcasted_iota(jnp.int32, (count, count), 1)
    return jnp.sum(jnp.where(at == to, jnp.broadcast_to(column, (count, count)), 0.0), axis=0, keepdims=True)


def one_hot(ids, experts, slots):
    me = lax.axis_index("expert")
    count = ids.shape[1]
    padded = max(8, experts)
    kinds = lax.broadcasted_iota(jnp.int32, (padded, count), 0)
    here = kinds == jnp.broadcast_to(ids, (padded, count))
    onehot = jnp.where(here, 1.0, 0.0)
    at = lax.broadcasted_iota(jnp.int32, (count, count), 0)
    to = lax.broadcasted_iota(jnp.int32, (count, count), 1)
    earlier = jnp.where(at < to, 1.0, 0.0).astype(BF)
    before = dot(onehot.astype(BF), earlier, 1, 0)
    position = jnp.sum(before * onehot, axis=0, keepdims=True).astype(jnp.int32)
    slot = (ids ^ me) * slots + position
    rows = experts * slots
    place = lax.broadcasted_iota(jnp.int32, (rows, count), 0)
    return jnp.where(place == jnp.broadcast_to(slot, (rows, count)), 1.0, 0.0).astype(BF)


def copy_in(sources, targets, sems):
    copies = [pltpu.make_async_copy(s, t, sems.at[k]) for k, (s, t) in enumerate(zip(sources, targets))]
    for copy in copies:
        copy.start()
    return copies


def tokens_body(experts, slots, ids_in, tokens_in, placed_out, *refs):
    blocks, (ids, tokens, sems) = refs[:experts], refs[experts:]
    copies = copy_in((ids_in, tokens_in), (ids, tokens), sems)
    copies[0].wait()
    placed = one_hot(ids[...], experts, slots)
    placed_out[...] = placed
    copies[1].wait()
    sent = dot(placed, tokens[...], 1, 0).astype(BF)
    for k in range(experts):
        blocks[k][...] = sent[k * slots:(k + 1) * slots]


def grads_body(experts, width, *refs):
    placed, *token_blocks = refs[:experts + 1]
    sources = refs[experts + 1:experts + 5]
    gate_up, down, *blocks = refs[experts + 5:-3]
    weight, out_grad, sems = refs[-3:]
    copies = copy_in(sources, (weight, out_grad, gate_up, down), sems)
    slots = token_blocks[0].shape[0]
    partner = lax.axis_index("dp") ^ PARTNER
    copies[0].wait()
    column = row_to_column(weight[...])
    copies[1].wait()
    scaled = (column * out_grad[...].astype(F32)).astype(BF)
    sent = dot(placed[...], scaled, 1, 0).astype(BF)
    for k in range(experts):
        blocks[k][...] = sent[k * slots:(k + 1) * slots]
    for k, half in enumerate(blocks[experts:]):
        columns_for(token_blocks[k], half, partner, width)
        columns_for(blocks[k], half, partner, width, len(MASKS) * width)
    copies[2].wait()
    copies[3].wait()


def columns_for(rows, out, device, width, start=0):
    for k, mask in enumerate(MASKS):
        at = pl.multiple_of((device ^ mask) * width, width)
        out[:, start + k * width:start + (k + 1) * width] = rows[:, pl.ds(at, width)]


def gather(blocks, rows):
    slots = blocks[0].shape[0]
    for k, block in enumerate(blocks):
        rows[k * slots:(k + 1) * slots, :] = block[...]


def forward_body(experts, width, *refs):
    blocks, (gate_up, pre_out, own, send, rows) = refs[:experts], refs[experts:]
    gather(blocks, rows)
    pre = dot(rows[...], gate_up[0], 1, 0)
    pre_out[...] = pre
    hidden = pre.shape[1] // 2
    gate, up = pre[:, :hidden], pre[:, hidden:]
    send[:, :hidden] = (gate * jax.nn.sigmoid(gate) * up).astype(BF)
    if width == 0:
        return
    device = lax.axis_index("dp")
    columns_for(rows, own, device, width)
    late = rows.shape[0] // 2
    for k, mask in enumerate(MASKS):
        at = pl.multiple_of((device ^ PARTNER ^ mask) * width, width)
        to, start = (k // 2) * late, hidden + (k % 2) * width
        send[to:to + late, start:start + width] = rows[late:, pl.ds(at, width)]


def backward_body(experts, width, *refs):
    blocks, (pre, down, own, send, d_gate, d_up, rows) = refs[:experts], refs[experts:]
    gather(blocks, rows)
    d_act = dot(rows[...], down[0], 1, 1)
    hidden = d_act.shape[1]
    gate, up = pre[:, :hidden], pre[:, hidden:]
    sig = jax.nn.sigmoid(gate)
    d_gate[...] = (d_act * up * sig * (1.0 + gate * (1.0 - sig))).astype(BF)
    d_up[...] = (d_act * (gate * sig)).astype(BF)
    if width == 0:
        return
    device = lax.axis_index("dp")
    columns_for(rows, own, device, width)
    late = rows.shape[0] // 2
    columns_for(rows.at[late:], send, device ^ PARTNER, width)


def return_body(experts, first, d_gate, d_up, gate_up, down, *blocks):
    slots = blocks[0].shape[0] // 2
    result = dot(first[:, :down.shape[1]], down[0], 1, 0).astype(BF)
    for k in range(experts):
        blocks[k][:slots] = result[k * slots:(k + 1) * slots]
    hidden = d_gate.shape[1]
    moved = dot(d_gate[...], gate_up[0, :, :hidden], 1, 1)
    moved = (moved + dot(d_up[...], gate_up[0, :, hidden:], 1, 1)).astype(BF)
    for k in range(experts):
        blocks[k][slots:] = moved[k * slots:(k + 1) * slots]


def terms_body(joined, hidden, *refs):
    halves, (own, factor, factor_in, late, kept, far, near, rows) = refs[:joined], refs[joined:]
    width, half = kept.shape[0], own.shape[1]
    slots, cut = halves[0].shape[0], rows.shape[0] // 2
    start = 0 if hidden else half
    for k, block in enumerate(halves):
        rows[k * slots:(k + 1) * slots, :] = block[:, start:start + half]
    if hidden:
        rows[cut:, :half // 2] = late[:cut, hidden:]
        rows[cut:, half // 2:] = late[cut:, hidden:]
    else:
        rows[cut:, :] = late[...]
    columns = kept.shape[1]
    for k, out in enumerate((kept, near.at[:width], far, near.at[width:])):
        at = slice(k * width, (k + 1) * width)
        total = dot(own[:, at], factor[:, :columns], 0, 0) + dot(rows[:, at], factor_in[:, :columns], 0, 0)
        out[...] = total.astype(out.dtype)


def pair_body(far, arrived, out):
    out[...] = (far[...] + arrived[far.shape[0]:, :].astype(F32)).astype(BF)


def total_of(kept, near, distant):
    return kept[...] + near[:kept.shape[0], :].astype(F32) + distant[...].astype(F32)


def early_body(*refs):
    first, second, (out, held, sems) = refs[:3], refs[3:6], refs[6:]
    width = held.shape[2]
    copies = []
    for k, terms in enumerate((first, second)):
        held[k] = total_of(*terms)
        target = out.at[:, pl.ds(2 * k * width, width)]
        copies.append(pltpu.make_async_copy(held.at[k], target, sems.at[k]))
        copies[k].start()
    for copy in copies:
        copy.wait()


def last_body(kept, near, distant, out_in, out, held, sem):
    held[...] = total_of(kept, near, distant)
    width = held.shape[1]
    copy = pltpu.make_async_copy(held, out.at[:, pl.ds(width, width)], sem)
    copy.start()
    copy.wait()


def combine_body(experts, *refs):
    blocks = refs[:experts]
    placed, weight, out_grad, mixed, token_grad, weight_out, rows = refs[experts:]
    slots = blocks[0].shape[0] // 2
    for k in range(experts):
        rows[k * slots:(k + 1) * slots, :] = blocks[k][:slots]
    copy_out = dot(placed[...], rows[...], 0, 0)
    mixed[...] = (row_to_column(weight[...]) * copy_out).astype(BF)
    products = jnp.sum(out_grad[...].astype(F32) * copy_out, axis=1, keepdims=True)
    weight_out[...] = column_to_row(products)
    for k in range(experts):
        rows[k * slots:(k + 1) * slots, :] = blocks[k][slots:]
    token_grad[...] = dot(placed[...], rows[...], 0, 0).astype(BF)


def permute(array, axis, size, step):
    return lax.ppermute(array, axis, [(i, i ^ step) for i in range(size)])


def exchange(blocks, axis, size, stride=1):
    return [blocks[0]] + [permute(blocks[k], axis, size, k * stride) for k in range(1, len(blocks))]


def across(block, k, experts, shards):
    pairs = [
        (i * experts + j, (i ^ PARTNER) * experts + (j ^ k)) for i in range(shards) for j in range(experts)
    ]
    return lax.ppermute(block, ("dp", "expert"), pairs)


def on_device(tokens, route_ids, route_weight, w_gate_up, w_down, out_grad):
    experts, shards = lax.axis_size("expert"), lax.axis_size("dp")
    count, top = route_ids.shape
    assert top == 1
    width = tokens.shape[1]
    hidden = w_down.shape[1]
    capacity = 3 * count // (2 * experts)
    slots = -(-capacity // 16) * 16
    rows = experts * slots
    share = width // shards
    staged = is_staged(width, shards)
    half = len(MASKS) * share if staged else 256
    ids = route_ids.reshape(1, count)
    weight = route_weight.reshape(1, count)

    block = shape((slots, width), BF)
    placed, *sent_tokens = call(
        functools.partial(tokens_body, experts, slots),
        [shape((rows, count), BF)] + [block] * experts, (ids, tokens),
        [pltpu.VMEM(a.shape, a.dtype) for a in (ids, tokens)] + [pltpu.SemaphoreType.DMA((2,))],
        flops=2 * rows * count * width, far_ins=(0, 1))
    token_blocks = exchange(sent_tokens, "expert", experts)
    joined = experts // 2 if staged else 0
    gate_up, down, *sent = call(
        functools.partial(grads_body, experts, share),
        [shape(w_gate_up.shape, BF), shape(w_down.shape, BF)] + [block] * experts
        + [shape((slots, 2 * half), BF)] * joined,
        (placed, *sent_tokens, weight, out_grad, w_gate_up, w_down),
        [pltpu.VMEM(a.shape, a.dtype) for a in (weight, out_grad)] + [pltpu.SemaphoreType.DMA((4,))],
        flops=2 * rows * count * width, far_ins=tuple(range(experts + 1, experts + 5)))
    grad_blocks = exchange(sent[:experts], "expert", experts)
    scratch = [pltpu.VMEM((rows, width), BF)]
    own_shape, late_shape = shape((rows, half), BF), shape((rows // 2, half), BF)
    piece = share if staged else 0
    pre, own_rows, first = call(
        functools.partial(forward_body, experts, piece),
        [shape((rows, 2 * hidden), F32), own_shape, shape((rows, hidden + half // 2), BF)],
        (*token_blocks, gate_up), scratch, flops=4 * rows * hidden * width)
    own_grads, late_grads, d_gate, d_up = call(
        functools.partial(backward_body, experts, piece),
        [own_shape, late_shape] + [shape((rows, hidden), BF)] * 2,
        (*grad_blocks, pre, down), scratch, flops=2 * rows * hidden * width)
    back = call(
        functools.partial(return_body, experts), [shape((2 * slots, width), BF)] * experts,
        (first, d_gate, d_up, gate_up, down), flops=6 * rows * hidden * width)
    if staged:
        first_in = permute(first, "dp", shards, PARTNER)
        both = [across(sent[experts + k], k, experts, shards) for k in range(joined)]
        late_in = permute(late_grads, "dp", shards, PARTNER)
        d_gate_in = permute(d_gate, "dp", shards, PARTNER)
        d_up_in = permute(d_up, "dp", shards, PARTNER)
        one = shape((share, hidden), F32)

        def summed(start, own, factor, factor_in, late):
            kept, far, near = call(
                functools.partial(terms_body, joined, start),
                [one, one, shape((2 * share, hidden), BF)], (*both, own, factor, factor_in, late),
                [pltpu.VMEM((rows, half), BF)], flops=4 * rows * hidden * half)
            near = permute(near, "dp", shards, MASKS[1])
            distant, = call(pair_body, [shape((share, hidden), BF)], (far, near))
            return kept, near, permute(distant, "dp", shards, MASKS[2])

        downs = summed(0, own_grads, first, first_in, late_in)
        gates = summed(hidden, own_rows, d_gate, d_gate_in, first_in)
        ups = summed(hidden, own_rows, d_up, d_up_in, first_in)
        whole = shape((share, 3 * hidden), F32)
        weight_grad, = call(
            early_body, [whole], (*gates, *downs),
            [pltpu.VMEM((2, share, hidden), F32), pltpu.SemaphoreType.DMA((2,))], far_outs=(0,))
        weight_grad, = call(
            last_body, [whole], (*ups, weight_grad),
            [pltpu.VMEM((share, hidden), F32), pltpu.SemaphoreType.DMA],
            far_ins=(3,), far_outs=(0,), aliases={3: 0})
    else:
        weight_grad = lax.psum_scatter(
            jnp.concatenate([
                dot(jnp.concatenate(token_blocks, axis=0), jnp.concatenate([d_gate, d_up], axis=1), 0, 0),
                dot(jnp.concatenate(grad_blocks, axis=0), first[:, :hidden], 0, 0)], axis=1),
            "dp", scatter_dimension=0, tiled=True)
    returned = exchange(back, "expert", experts)
    mixed, token_grad, weight_row = call(
        functools.partial(combine_body, experts),
        [shape((count, width), BF), shape((count, width), BF), shape((1, count), F32)],
        (*returned, placed, weight, out_grad), scratch, flops=4 * rows * count * width)
    return (mixed, token_grad, weight_row.reshape(count, 1), weight_grad[None])


def is_staged(width, shards):
    return shards == 8 and (width // shards) % 128 == 0


PARTNER = 2
MASKS = (0, 1, 4, 5)


def solution(mesh):
    split = P(("dp", "expert"), None)
    whole = P("expert", None, None)

    return jax.shard_map(
        on_device,
        mesh=mesh,
        in_specs=(split, split, split, whole, whole, split),
        out_specs=(split, split, split, P("expert", "dp", None)),
        check_vma=False,
    )
```

profile of v0, /device:TPU:0, one launch (start us, length us, event | category | flops | bytes accessed | tf_op | source)
XLA Modules:
  0.0 53.9 jit_solution(2225029010378503)
XLA Ops:
  0.6 1.2 %shard_map.93 = (bf16[192,128]{1,0:T(8,128)(2,1)S(1)}, bf16[48,1024]{1,0:T(8,128)(2,1)S(1)}, bf16[48,1024]{1,0:T(8,128)(2,1)S(1)}, bf16[48,1024]{1,0:T(8,128)(2,1)S(1)}, bf16[48,1024]{1,0:T(8,128)(2,1)S(1)}) custom-call(s32[1,128]{1,0:T(1,128)} %bitcast.7, bf16[128,1024]{1,0:T(8,128)(2,1)} %tokens_in.1), custom_call_target="tpu_custom_call" | custom-call | flops 50331648 | bytes 705024 | tf_op jit(solution)/shard_map/pallas_call | solution.py:27
  1.9 0.6 %collective-permute-start = (bf16[48,1024]{1,0:T(8,128)(2,1)S(1)}, bf16[48,1024]{1,0:T(8,128)(2,1)S(1)}, u32[]{:S(2)}, u32[]{:S(2)}) collective-permute-start(bf16[48,1024]{1,0:T(8,128)(2,1)S(1)} %get-tuple-element.41.refs_2_), channel_id=1, source_target_pairs={{0,1},{1,0},{2,3},{3,2},{4,5},{5,4},{6,7},{7,6},{8,9},{9,8},{10,11... | collective-permute-start | bytes 294920 | tf_op jit(solution)/shard_map/ppermute | solution.py:240
  2.4 2.6 %collective-permute-start.1 = (bf16[48,1024]{1,0:T(8,128)(2,1)S(1)}, bf16[48,1024]{1,0:T(8,128)(2,1)S(1)}, u32[]{:S(2)}, u32[]{:S(2)}) collective-permute-start(bf16[48,1024]{1,0:T(8,128)(2,1)S(1)} %get-tuple-element.42.refs_3_), channel_id=1, source_target_pairs={{0,2},{1,3},{2,0},{3,1},{4,6},{5,7},{6,4},{7,5},{8,10},{9,11},{10,... | collective-permute-start | bytes 294920 | tf_op jit(solution)/shard_map/ppermute | solution.py:240
  5.0 0.0 collective-permute-start.2
  5.0 1.7 %shard_map.94 = (bf16[1,1024,768]{2,1,0:T(8,128)(2,1)S(1)}, bf16[1,384,1024]{2,1,0:T(8,128)(2,1)S(1)}, bf16[48,1024]{1,0:T(8,128)(2,1)S(1)}, bf16[48,1024]{1,0:T...) custom-call(bf16[192,128]{1,0:T(8,128)(2,1)S(1)} %get-tuple-element., ...), custom_call_target="tpu_custom_call" | custom-call | flops 50331648 | bytes 6013440 | tf_op jit(solution)/shard_map/pallas_call | solution.py:27
  6.8 1.9 %collective-permute-done.1.refs_2_ = bf16[48,1024]{1,0:T(8,128)(2,1)S(1)} collective-permute-done((bf16[48,1024]{1,0:T(8,128)(2,1)S(1)}, bf16[48,1024]{1,0:T(8,128)(2,1)S(1)}, u32[]{:S(2)}, u32[]{:S(2)}) %collective-permute-start.1) | collective-permute-done | bytes 98336 | tf_op jit(solution)/shard_map/ppermute | solution.py:240
  8.6 1.6 %collective-permute-done.2.refs_3_ = bf16[48,1024]{1,0:T(8,128)(2,1)S(1)} collective-permute-done((bf16[48,1024]{1,0:T(8,128)(2,1)S(1)}, bf16[48,1024]{1,0:T(8,128)(2,1)S(1)}, u32[]{:S(2)}, u32[]{:S(2)}) %collective-permute-start.2) | collective-permute-done | bytes 98336 | tf_op jit(solution)/shard_map/ppermute | solution.py:240
  10.2 0.5 %shard_map.95 = (f32[192,768]{1,0:T(8,128)S(1)}, bf16[192,512]{1,0:T(8,128)(2,1)S(1)}, bf16[192,640]{1,0:T(8,128)(2,1)S(1)}) custom-call(bf16[48,1024]{1,0:T(8,128)(2,1)S(1)} %get-tuple-element.40.refs_1_.refs_0_, bf16[48,1024]{1,0:T(8,128)(2,1)S(1)} %collective-permute-done.refs_1_, bf16[48,1024]{1,0:T(8,128)(2,1)S(1)} %collective-permute-done.1.refs_2_, ...), custom_call_target="tpu_custom_call" | custom-call | flops 301989888 | bytes 2998272 | tf_op jit(solution)/shard_map/pallas_call | solution.py:27
  10.8 1.6 %collective-permute-start.12 = (bf16[192,640]{1,0:T(8,128)(2,1)S(1)}, bf16[192,640]{1,0:T(8,128)(2,1)S(1)}, u32[]{:S(2)}, u32[]{:S(2)}) collective-permute-start(bf16[192,640]{1,0:T(8,128)(2,1)S(1)} %get-tuple-element.46.first.refs_3_), channel_id=1, source_target_pairs={{0,8},{4,12},{8,0},{12,4},{16,24},{20,28},{24,16},{28,20},{1,9},{5... | collective-permute-start | bytes 737288 | tf_op jit(solution)/shard_map/ppermute | solution.py:240
  12.4 0.1 collective-permute-start.3
  12.5 1.5 %collective-permute-start.4 = (bf16[48,1024]{1,0:T(8,128)(2,1)S(1)}, bf16[48,1024]{1,0:T(8,128)(2,1)S(1)}, u32[]{:S(2)}, u32[]{:S(2)}) collective-permute-start(bf16[48,1024]{1,0:T(8,128)(2,1)S(1)} %get-tuple-element.49), channel_id=1, source_target_pairs={{0,2},{1,3},{2,0},{3,1},{4,6},{5,7},{6,4},{7,5},{8,10},{9,11},{10,... | collective-permute-start | bytes 294920 | tf_op jit(solution)/shard_map/ppermute | solution.py:240
  14.0 0.3 collective-permute-start.5
  14.2 0.5 collective-permute-start.9
  14.7 1.2 %collective-permute-start.10 = (bf16[48,1024]{1,0:T(8,128)(2,1)S(1)}, bf16[48,1024]{1,0:T(8,128)(2,1)S(1)}, u32[]{:S(2)}, u32[]{:S(2)}) collective-permute-start(bf16[48,1024]{1,0:T(8,128)(2,1)S(1)} %get-tuple-element.63), channel_id=1, source_target_pairs={{0,9},{1,8},{2,11},{3,10},{4,13},{5,12},{6,15},{7,14},{8,1},{9,0},... | collective-permute-start | bytes 294920 | tf_op jit(solution)/shard_map/ppermute | solution.py:251
  16.0 2.2 %collective-permute-done.4.refs_2_ = bf16[48,1024]{1,0:T(8,128)(2,1)S(1)} collective-permute-done((bf16[48,1024]{1,0:T(8,128)(2,1)S(1)}, bf16[48,1024]{1,0:T(8,128)(2,1)S(1)}, u32[]{:S(2)}, u32[]{:S(2)}) %collective-permute-start.4) | collective-permute-done | bytes 98336 | tf_op jit(solution)/shard_map/ppermute | solution.py:240
  18.1 1.0 %collective-permute-done.5.refs_3_ = bf16[48,1024]{1,0:T(8,128)(2,1)S(1)} collective-permute-done((bf16[48,1024]{1,0:T(8,128)(2,1)S(1)}, bf16[48,1024]{1,0:T(8,128)(2,1)S(1)}, u32[]{:S(2)}, u32[]{:S(2)}) %collective-permute-start.5) | collective-permute-done | bytes 98336 | tf_op jit(solution)/shard_map/ppermute | solution.py:240
  19.2 0.5 shard_map.96
  19.7 0.6 %collective-permute-start.18 = (bf16[96,512]{1,0:T(8,128)(2,1)S(1)}, bf16[96,512]{1,0:T(8,128)(2,1)S(1)}, u32[]{:S(2)}, u32[]{:S(2)}) collective-permute-start(bf16[96,512]{1,0:T(8,128)(2,1)S(1)} %get-tuple-element.72), channel_id=1, source_target_pairs={{0,8},{4,12},{8,0},{12,4},{16,24},{20,28},{24,16},{28,20},{1,9},{5... | collective-permute-start | bytes 294920 | tf_op jit(solution)/shard_map/ppermute | solution.py:240
  20.3 1.5 %collective-permute-start.15 = (bf16[192,384]{1,0:T(8,128)(2,1)S(1)}, bf16[192,384]{1,0:T(8,128)(2,1)S(1)}, u32[]{:S(2)}, u32[]{:S(2)}) collective-permute-start(bf16[192,384]{1,0:T(8,128)(2,1)S(1)} %get-tuple-element.53.d_gate.refs_3_), channel_id=1, source_target_pairs={{0,8},{4,12},{8,0},{12,4},{16,24},{20,28},{24,16},{28,20},{1,9},{5... | collective-permute-start | bytes 442376 | tf_op jit(solution)/shard_map/ppermute | solution.py:240
  21.8 0.0 collective-permute-done.9.refs_0_
  21.8 1.5 %collective-permute-start.11 = (bf16[192,384]{1,0:T(8,128)(2,1)S(1)}, bf16[192,384]{1,0:T(8,128)(2,1)S(1)}, u32[]{:S(2)}, u32[]{:S(2)}) collective-permute-start(bf16[192,384]{1,0:T(8,128)(2,1)S(1)} %get-tuple-element.54.d_up.refs_3_), channel_id=1, source_target_pairs={{0,8},{4,12},{8,0},{12,4},{16,24},{20,28},{24,16},{28,20},{1,9},{5... | collective-permute-start | bytes 442376 | tf_op jit(solution)/shard_map/ppermute | solution.py:240
  23.3 2.1 %collective-permute-done.18.refs_5_ = bf16[96,512]{1,0:T(8,128)(2,1)S(1)} collective-permute-done((bf16[96,512]{1,0:T(8,128)(2,1)S(1)}, bf16[96,512]{1,0:T(8,128)(2,1)S(1)}, u32[]{:S(2)}, u32[]{:S(2)}) %collective-permute-start.18) | collective-permute-done | bytes 98336 | tf_op jit(solution)/shard_map/ppermute | solution.py:240
  25.4 0.5 shard_map.103
  25.9 1.8 %collective-permute-start.19 = (bf16[256,384]{1,0:T(8,128)(2,1)S(1)}, bf16[256,384]{1,0:T(8,128)(2,1)S(1)}, u32[]{:S(2)}, u32[]{:S(2)}) collective-permute-start(bf16[256,384]{1,0:T(8,128)(2,1)S(1)} %get-tuple-element.74), channel_id=1, source_target_pairs={{0,4},{4,0},{8,12},{12,8},{16,20},{20,16},{24,28},{28,24},{1,5},{5... | collective-permute-start | bytes 589832 | tf_op jit(solution)/shard_map/ppermute | solution.py:240
  27.7 0.9 %collective-permute-done.15.refs_4_ = bf16[192,384]{1,0:T(8,128)(2,1)S(1)} collective-permute-done((bf16[192,384]{1,0:T(8,128)(2,1)S(1)}, bf16[192,384]{1,0:T(8,128)(2,1)S(1)}, u32[]{:S(2)}, u32[]{:S(2)}) %collective-permute-start.15) | collective-permute-done | bytes 147488 | tf_op jit(solution)/shard_map/ppermute | solution.py:240
  28.6 0.5 shard_map.101
  29.0 1.8 %collective-permute-start.16 = (bf16[256,384]{1,0:T(8,128)(2,1)S(1)}, bf16[256,384]{1,0:T(8,128)(2,1)S(1)}, u32[]{:S(2)}, u32[]{:S(2)}) collective-permute-start(bf16[256,384]{1,0:T(8,128)(2,1)S(1)} %get-tuple-element.69), channel_id=1, source_target_pairs={{0,4},{4,0},{8,12},{12,8},{16,20},{20,16},{24,28},{28,24},{1,5},{5... | collective-permute-start | bytes 589832 | tf_op jit(solution)/shard_map/ppermute | solution.py:240
  30.8 0.7 %collective-permute-done.11.refs_4_ = bf16[192,384]{1,0:T(8,128)(2,1)S(1)} collective-permute-done((bf16[192,384]{1,0:T(8,128)(2,1)S(1)}, bf16[192,384]{1,0:T(8,128)(2,1)S(1)}, u32[]{:S(2)}, u32[]{:S(2)}) %collective-permute-start.11) | collective-permute-done | bytes 147488 | tf_op jit(solution)/shard_map/ppermute | solution.py:240
  31.5 0.5 shard_map.99
  32.0 0.0 copy-start
  32.0 0.0 copy-start.1
  32.0 1.7 %collective-permute-start.13 = (bf16[256,384]{1,0:T(8,128)(2,1)S(1)}, bf16[256,384]{1,0:T(8,128)(2,1)S(1)}, u32[]{:S(2)}, u32[]{:S(2)}) collective-permute-start(bf16[256,384]{1,0:T(8,128)(2,1)S(1)} %get-tuple-element.66), channel_id=1, source_target_pairs={{0,4},{4,0},{8,12},{12,8},{16,20},{20,16},{24,28},{28,24},{1,5},{5... | collective-permute-start | bytes 589832 | tf_op jit(solution)/shard_map/ppermute | solution.py:240
  33.8 0.9 %shard_map.97 = (bf16[96,1024]{1,0:T(8,128)(2,1)S(1)}, bf16[96,1024]{1,0:T(8,128)(2,1)S(1)}, bf16[96,1024]{1,0:T(8,128)(2,1)S(1)}, bf16[96,1024]{1,0:T(8,128)(2,1)S(1)}) custom-call(bf16[192,640]{1,0:T(8,128)(2,1)S(1)} %get-tuple-element.46.first.refs_3_, bf16[192,384]{1,0:T(8,128)(2,1)S(1)} %get-tuple-element.53.d_gate.refs_3_, ...), custom_call_target="tpu_custom_call" | custom-call | flops 452984832 | bytes 3686400 | tf_op jit(solution)/shard_map/pallas_call | solution.py:27
  34.7 0.1 collective-permute-start.6
  34.8 1.6 %collective-permute-start.7 = (bf16[96,1024]{1,0:T(8,128)(2,1)S(1)}, bf16[96,1024]{1,0:T(8,128)(2,1)S(1)}, u32[]{:S(2)}, u32[]{:S(2)}) collective-permute-start(bf16[96,1024]{1,0:T(8,128)(2,1)S(1)} %get-tuple-element.57), channel_id=1, source_target_pairs={{0,2},{1,3},{2,0},{3,1},{4,6},{5,7},{6,4},{7,5},{8,10},{9,11},{10,... | collective-permute-start | bytes 589832 | tf_op jit(solution)/shard_map/ppermute | solution.py:240
  36.3 0.3 collective-permute-start.8
  36.6 1.1 %collective-permute-done.16.arrived.refs_1_ = bf16[256,384]{1,0:T(8,128)(2,1)S(1)} collective-permute-done((bf16[256,384]{1,0:T(8,128)(2,1)S(1)}, bf16[256,384]{1,0:T(8,128)(2,1)S(1)}, u32[]{:S(2)}, u32[]{:S(2)}) %collective-permute-start.16) | collective-permute-done | bytes 196640 | tf_op jit(solution)/shard_map/ppermute | solution.py:240
  37.7 2.7 %collective-permute-start.20 = (bf16[128,384]{1,0:T(8,128)(2,1)S(1)}, bf16[128,384]{1,0:T(8,128)(2,1)S(1)}, u32[]{:S(2)}, u32[]{:S(2)}) collective-permute-start(bf16[128,384]{1,0:T(8,128)(2,1)S(1)} %shard_map.104), channel_id=1, source_target_pairs={{0,16},{4,20},{8,24},{12,28},{16,0},{20,4},{24,8},{28,12},{1,17},{... | collective-permute-start | bytes 294920 | tf_op jit(solution)/shard_map/ppermute | solution.py:240
  40.4 0.4 collective-permute-done.13.arrived.near
  40.9 2.7 %collective-permute-start.17 = (bf16[128,384]{1,0:T(8,128)(2,1)S(1)}, bf16[128,384]{1,0:T(8,128)(2,1)S(1)}, u32[]{:S(2)}, u32[]{:S(2)}) collective-permute-start(bf16[128,384]{1,0:T(8,128)(2,1)S(1)} %shard_map.102), channel_id=1, source_target_pairs={{0,16},{4,20},{8,24},{12,28},{16,0},{20,4},{24,8},{28,12},{1,17},{... | collective-permute-start | bytes 294920 | tf_op jit(solution)/shard_map/ppermute | solution.py:240
  43.6 0.3 collective-permute-start.14
  43.9 1.8 %collective-permute-done.8.refs_3_ = bf16[96,1024]{1,0:T(8,128)(2,1)S(1)} collective-permute-done((bf16[96,1024]{1,0:T(8,128)(2,1)S(1)}, bf16[96,1024]{1,0:T(8,128)(2,1)S(1)}, u32[]{:S(2)}, u32[]{:S(2)}) %collective-permute-start.8) | collective-permute-done | bytes 196640 | tf_op jit(solution)/shard_map/ppermute | solution.py:240
  45.7 1.1 %shard_map.98 = (bf16[128,1024]{1,0:T(8,128)(2,1)}, bf16[128,1024]{1,0:T(8,128)(2,1)}, f32[1,128]{1,0:T(1,128)}) custom-call(bf16[96,1024]{1,0:T(8,128)(2,1)S(1)} %get-tuple-element.55.refs_0_, bf16[96,1024]{1,0:T(8,128)(2,1)S(1)} %collective-permute-done.6.refs_1_, bf16[96,1024]{1,0:T(8,128)(2,1)S(1)} %collective-permute-done.7.refs_2_, ...), custom_call_target="tpu_custom_call" | custom-call | flops 100663296 | bytes 1623040 | tf_op jit(solution)/shard_map/pallas_call | solution.py:27
  46.9 1.8 %collective-permute-done.20.refs_5_ = bf16[128,384]{1,0:T(8,128)(2,1)S(1)} collective-permute-done((bf16[128,384]{1,0:T(8,128)(2,1)S(1)}, bf16[128,384]{1,0:T(8,128)(2,1)S(1)}, u32[]{:S(2)}, u32[]{:S(2)}) %collective-permute-start.20) | collective-permute-done | bytes 98336 | tf_op jit(solution)/shard_map/ppermute | solution.py:240
  48.7 3.2 %collective-permute-done.17.refs_2_ = bf16[128,384]{1,0:T(8,128)(2,1)S(1)} collective-permute-done((bf16[128,384]{1,0:T(8,128)(2,1)S(1)}, bf16[128,384]{1,0:T(8,128)(2,1)S(1)}, u32[]{:S(2)}, u32[]{:S(2)}) %collective-permute-start.17) | collective-permute-done | bytes 98336 | tf_op jit(solution)/shard_map/ppermute | solution.py:240
  51.8 0.8 %shard_map.105.out_in = f32[128,1152]{1,0:T(8,128)} custom-call(f32[128,384]{1,0:T(8,128)S(1)} %get-tuple-element.68.refs_0_, bf16[256,384]{1,0:T(8,128)(2,1)S(1)} %collective-permute-done.16.arrived.refs_1_, bf16[128,384]{1,0:T(8,128)(2,1)S(1)} %collective-permute-done.17.refs_2_, f32[128,384]{1,0:T(8,128)S(1)} %get-tuple-element.73.refs_3_, ...), custom_call_target="tpu_custom_call" | custom-call | bytes 1572864 | tf_op jit(solution)/shard_map/pallas_call | solution.py:27
  52.6 0.6 %collective-permute-done.14.distant = bf16[128,384]{1,0:T(8,128)(2,1)S(1)} collective-permute-done((bf16[128,384]{1,0:T(8,128)(2,1)S(1)}, bf16[128,384]{1,0:T(8,128)(2,1)S(1)}, u32[]{:S(2)}, u32[]{:S(2)}) %collective-permute-start.14) | collective-permute-done | bytes 98336 | tf_op jit(solution)/shard_map/ppermute | solution.py:240
  53.2 0.7 %shard_map.106 = f32[128,1152]{1,0:T(8,128)} custom-call(f32[128,384]{1,0:T(8,128)S(1)} %get-tuple-element.65.kept, bf16[256,384]{1,0:T(8,128)(2,1)S(1)} %collective-permute-done.13.arrived.near, bf16[128,384]{1,0:T(8,128)(2,1)S(1)} %collective-permute-done.14.distant, f32[128,1152]{1,0:T(8,128)} %shard_map.105.out_in), custom_call_target="tpu_custom_call", output_to_operand_aliasing={{}: (3, {})} | custom-call | bytes 1671168 | tf_op jit(solution)/shard_map/pallas_call | solution.py:27
  (12 shorter events, 0.1 us)
Async XLA Ops:
  1.9 4.9 %collective-permute-start = (bf16[48,1024]{1,0:T(8,128)(2,1)S(1)}, bf16[48,1024]{1,0:T(8,128)(2,1)S(1)}, u32[]{:S(2)}, u32[]{:S(2)}) collective-permute-start(bf16[48,1024]{1,0:T(8,128)(2,1)S(1)} %get-tuple-element.41.refs_2_), channel_id=1, source_target_pairs={{0,1},{1,0},{2,3},{3,2},{4,5},{5,4},{6,7},{7,6},{8,9},{9,8},{10,11... | collective-permute-start | bytes 294920 | tf_op jit(solution)/shard_map/ppermute | solution.py:240
  2.4 6.2 %collective-permute-start.1 = (bf16[48,1024]{1,0:T(8,128)(2,1)S(1)}, bf16[48,1024]{1,0:T(8,128)(2,1)S(1)}, u32[]{:S(2)}, u32[]{:S(2)}) collective-permute-start(bf16[48,1024]{1,0:T(8,128)(2,1)S(1)} %get-tuple-element.42.refs_3_), channel_id=1, source_target_pairs={{0,2},{1,3},{2,0},{3,1},{4,6},{5,7},{6,4},{7,5},{8,10},{9,11},{10,... | collective-permute-start | bytes 294920 | tf_op jit(solution)/shard_map/ppermute | solution.py:240
  5.0 5.2 %collective-permute-start.2 = (bf16[48,1024]{1,0:T(8,128)(2,1)S(1)}, bf16[48,1024]{1,0:T(8,128)(2,1)S(1)}, u32[]{:S(2)}, u32[]{:S(2)}) collective-permute-start(bf16[48,1024]{1,0:T(8,128)(2,1)S(1)} %get-tuple-element.43.refs_4_), channel_id=1, source_target_pairs={{0,3},{1,2},{2,1},{3,0},{4,7},{5,6},{6,5},{7,4},{8,11},{9,10},{10,... | collective-permute-start | bytes 294920 | tf_op jit(solution)/shard_map/ppermute | solution.py:240
  10.8 14.6 %collective-permute-start.12 = (bf16[192,640]{1,0:T(8,128)(2,1)S(1)}, bf16[192,640]{1,0:T(8,128)(2,1)S(1)}, u32[]{:S(2)}, u32[]{:S(2)}) collective-permute-start(bf16[192,640]{1,0:T(8,128)(2,1)S(1)} %get-tuple-element.46.first.refs_3_), channel_id=1, source_target_pairs={{0,8},{4,12},{8,0},{12,4},{16,24},{20,28},{24,16},{28,20},{1,9},{5... | collective-permute-start | bytes 737288 | tf_op jit(solution)/shard_map/ppermute | solution.py:240
  12.4 2.3 %collective-permute-start.3 = (bf16[48,1024]{1,0:T(8,128)(2,1)S(1)}, bf16[48,1024]{1,0:T(8,128)(2,1)S(1)}, u32[]{:S(2)}, u32[]{:S(2)}) collective-permute-start(bf16[48,1024]{1,0:T(8,128)(2,1)S(1)} %get-tuple-element.48), channel_id=1, source_target_pairs={{0,1},{1,0},{2,3},{3,2},{4,5},{5,4},{6,7},{7,6},{8,9},{9,8},{10,11... | collective-permute-start | bytes 294920 | tf_op jit(solution)/shard_map/ppermute | solution.py:240
  12.5 5.7 %collective-permute-start.4 = (bf16[48,1024]{1,0:T(8,128)(2,1)S(1)}, bf16[48,1024]{1,0:T(8,128)(2,1)S(1)}, u32[]{:S(2)}, u32[]{:S(2)}) collective-permute-start(bf16[48,1024]{1,0:T(8,128)(2,1)S(1)} %get-tuple-element.49), channel_id=1, source_target_pairs={{0,2},{1,3},{2,0},{3,1},{4,6},{5,7},{6,4},{7,5},{8,10},{9,11},{10,... | collective-permute-start | bytes 294920 | tf_op jit(solution)/shard_map/ppermute | solution.py:240
  14.0 5.2 %collective-permute-start.5 = (bf16[48,1024]{1,0:T(8,128)(2,1)S(1)}, bf16[48,1024]{1,0:T(8,128)(2,1)S(1)}, u32[]{:S(2)}, u32[]{:S(2)}) collective-permute-start(bf16[48,1024]{1,0:T(8,128)(2,1)S(1)} %get-tuple-element.50), channel_id=1, source_target_pairs={{0,3},{1,2},{2,1},{3,0},{4,7},{5,6},{6,5},{7,4},{8,11},{9,10},{10,... | collective-permute-start | bytes 294920 | tf_op jit(solution)/shard_map/ppermute | solution.py:240
  14.2 7.5 %collective-permute-start.9 = (bf16[48,1024]{1,0:T(8,128)(2,1)S(1)}, bf16[48,1024]{1,0:T(8,128)(2,1)S(1)}, u32[]{:S(2)}, u32[]{:S(2)}) collective-permute-start(bf16[48,1024]{1,0:T(8,128)(2,1)S(1)} %get-tuple-element.62), channel_id=1, source_target_pairs={{0,8},{1,9},{2,10},{3,11},{4,12},{5,13},{6,14},{7,15},{8,0},{9,1},... | collective-permute-start | bytes 294920 | tf_op jit(solution)/shard_map/ppermute | solution.py:251
  14.7 8.6 %collective-permute-start.10 = (bf16[48,1024]{1,0:T(8,128)(2,1)S(1)}, bf16[48,1024]{1,0:T(8,128)(2,1)S(1)}, u32[]{:S(2)}, u32[]{:S(2)}) collective-permute-start(bf16[48,1024]{1,0:T(8,128)(2,1)S(1)} %get-tuple-element.63), channel_id=1, source_target_pairs={{0,9},{1,8},{2,11},{3,10},{4,13},{5,12},{6,15},{7,14},{8,1},{9,0},... | collective-permute-start | bytes 294920 | tf_op jit(solution)/shard_map/ppermute | solution.py:251
  19.7 5.7 %collective-permute-start.18 = (bf16[96,512]{1,0:T(8,128)(2,1)S(1)}, bf16[96,512]{1,0:T(8,128)(2,1)S(1)}, u32[]{:S(2)}, u32[]{:S(2)}) collective-permute-start(bf16[96,512]{1,0:T(8,128)(2,1)S(1)} %get-tuple-element.72), channel_id=1, source_target_pairs={{0,8},{4,12},{8,0},{12,4},{16,24},{20,28},{24,16},{28,20},{1,9},{5... | collective-permute-start | bytes 294920 | tf_op jit(solution)/shard_map/ppermute | solution.py:240
  20.3 8.3 %collective-permute-start.15 = (bf16[192,384]{1,0:T(8,128)(2,1)S(1)}, bf16[192,384]{1,0:T(8,128)(2,1)S(1)}, u32[]{:S(2)}, u32[]{:S(2)}) collective-permute-start(bf16[192,384]{1,0:T(8,128)(2,1)S(1)} %get-tuple-element.53.d_gate.refs_3_), channel_id=1, source_target_pairs={{0,8},{4,12},{8,0},{12,4},{16,24},{20,28},{24,16},{28,20},{1,9},{5... | collective-permute-start | bytes 442376 | tf_op jit(solution)/shard_map/ppermute | solution.py:240
  21.8 9.7 %collective-permute-start.11 = (bf16[192,384]{1,0:T(8,128)(2,1)S(1)}, bf16[192,384]{1,0:T(8,128)(2,1)S(1)}, u32[]{:S(2)}, u32[]{:S(2)}) collective-permute-start(bf16[192,384]{1,0:T(8,128)(2,1)S(1)} %get-tuple-element.54.d_up.refs_3_), channel_id=1, source_target_pairs={{0,8},{4,12},{8,0},{12,4},{16,24},{20,28},{24,16},{28,20},{1,9},{5... | collective-permute-start | bytes 442376 | tf_op jit(solution)/shard_map/ppermute | solution.py:240
  25.9 10.4 %collective-permute-start.19 = (bf16[256,384]{1,0:T(8,128)(2,1)S(1)}, bf16[256,384]{1,0:T(8,128)(2,1)S(1)}, u32[]{:S(2)}, u32[]{:S(2)}) collective-permute-start(bf16[256,384]{1,0:T(8,128)(2,1)S(1)} %get-tuple-element.74), channel_id=1, source_target_pairs={{0,4},{4,0},{8,12},{12,8},{16,20},{20,16},{24,28},{28,24},{1,5},{5... | collective-permute-start | bytes 589832 | tf_op jit(solution)/shard_map/ppermute | solution.py:240
  29.0 8.7 %collective-permute-start.16 = (bf16[256,384]{1,0:T(8,128)(2,1)S(1)}, bf16[256,384]{1,0:T(8,128)(2,1)S(1)}, u32[]{:S(2)}, u32[]{:S(2)}) collective-permute-start(bf16[256,384]{1,0:T(8,128)(2,1)S(1)} %get-tuple-element.69), channel_id=1, source_target_pairs={{0,4},{4,0},{8,12},{12,8},{16,20},{20,16},{24,28},{28,24},{1,5},{5... | collective-permute-start | bytes 589832 | tf_op jit(solution)/shard_map/ppermute | solution.py:240
  32.0 13.7 %copy-start = (bf16[128,1024]{1,0:T(8,128)(2,1)S(1)}, bf16[128,1024]{1,0:T(8,128)(2,1)}, u32[]{:S(2)}) copy-start(bf16[128,1024]{1,0:T(8,128)(2,1)} %refs_6_.3) | copy-start | bytes 786436
  32.0 13.7 %copy-start.1 = (f32[128,1]{0,1:T(1,128)S(1)}, f32[128,1]{0,1:T(1,128)}, u32[]{:S(2)}) copy-start(f32[128,1]{0,1:T(1,128)} %param.8) | copy-start | bytes 1540
  32.0 8.9 %collective-permute-start.13 = (bf16[256,384]{1,0:T(8,128)(2,1)S(1)}, bf16[256,384]{1,0:T(8,128)(2,1)S(1)}, u32[]{:S(2)}, u32[]{:S(2)}) collective-permute-start(bf16[256,384]{1,0:T(8,128)(2,1)S(1)} %get-tuple-element.66), channel_id=1, source_target_pairs={{0,4},{4,0},{8,12},{12,8},{16,20},{20,16},{24,28},{28,24},{1,5},{5... | collective-permute-start | bytes 589832 | tf_op jit(solution)/shard_map/ppermute | solution.py:240
  34.7 8.9 %collective-permute-start.6 = (bf16[96,1024]{1,0:T(8,128)(2,1)S(1)}, bf16[96,1024]{1,0:T(8,128)(2,1)S(1)}, u32[]{:S(2)}, u32[]{:S(2)}) collective-permute-start(bf16[96,1024]{1,0:T(8,128)(2,1)S(1)} %get-tuple-element.56), channel_id=1, source_target_pairs={{0,1},{1,0},{2,3},{3,2},{4,5},{5,4},{6,7},{7,6},{8,9},{9,8},{10,11... | collective-permute-start | bytes 589832 | tf_op jit(solution)/shard_map/ppermute | solution.py:240
  34.8 9.2 %collective-permute-start.7 = (bf16[96,1024]{1,0:T(8,128)(2,1)S(1)}, bf16[96,1024]{1,0:T(8,128)(2,1)S(1)}, u32[]{:S(2)}, u32[]{:S(2)}) collective-permute-start(bf16[96,1024]{1,0:T(8,128)(2,1)S(1)} %get-tuple-element.57), channel_id=1, source_target_pairs={{0,2},{1,3},{2,0},{3,1},{4,6},{5,7},{6,4},{7,5},{8,10},{9,11},{10,... | collective-permute-start | bytes 589832 | tf_op jit(solution)/shard_map/ppermute | solution.py:240
  36.3 9.4 %collective-permute-start.8 = (bf16[96,1024]{1,0:T(8,128)(2,1)S(1)}, bf16[96,1024]{1,0:T(8,128)(2,1)S(1)}, u32[]{:S(2)}, u32[]{:S(2)}) collective-permute-start(bf16[96,1024]{1,0:T(8,128)(2,1)S(1)} %get-tuple-element.58), channel_id=1, source_target_pairs={{0,3},{1,2},{2,1},{3,0},{4,7},{5,6},{6,5},{7,4},{8,11},{9,10},{10,... | collective-permute-start | bytes 589832 | tf_op jit(solution)/shard_map/ppermute | solution.py:240
  37.7 11.0 %collective-permute-start.20 = (bf16[128,384]{1,0:T(8,128)(2,1)S(1)}, bf16[128,384]{1,0:T(8,128)(2,1)S(1)}, u32[]{:S(2)}, u32[]{:S(2)}) collective-permute-start(bf16[128,384]{1,0:T(8,128)(2,1)S(1)} %shard_map.104), channel_id=1, source_target_pairs={{0,16},{4,20},{8,24},{12,28},{16,0},{20,4},{24,8},{28,12},{1,17},{... | collective-permute-start | bytes 294920 | tf_op jit(solution)/shard_map/ppermute | solution.py:240
  40.9 11.0 %collective-permute-start.17 = (bf16[128,384]{1,0:T(8,128)(2,1)S(1)}, bf16[128,384]{1,0:T(8,128)(2,1)S(1)}, u32[]{:S(2)}, u32[]{:S(2)}) collective-permute-start(bf16[128,384]{1,0:T(8,128)(2,1)S(1)} %shard_map.102), channel_id=1, source_target_pairs={{0,16},{4,20},{8,24},{12,28},{16,0},{20,4},{24,8},{28,12},{1,17},{... | collective-permute-start | bytes 294920 | tf_op jit(solution)/shard_map/ppermute | solution.py:240
  43.6 9.6 %collective-permute-start.14 = (bf16[128,384]{1,0:T(8,128)(2,1)S(1)}, bf16[128,384]{1,0:T(8,128)(2,1)S(1)}, u32[]{:S(2)}, u32[]{:S(2)}) collective-permute-start(bf16[128,384]{1,0:T(8,128)(2,1)S(1)} %shard_map.100), channel_id=1, source_target_pairs={{0,16},{4,20},{8,24},{12,28},{16,0},{20,4},{24,8},{28,12},{1,17},{... | collective-permute-start | bytes 294920 | tf_op jit(solution)/shard_map/ppermute | solution.py:240
where the time goes:
time: 54.1 us; the launch traced here: 53.9 us
  starting transfers between devices  24.9 us (46%)
  waiting for transfers between devices  19.2 us (35%)
  Pallas kernels  9.06 us (17%)
  between operations  0.77 us (1%)
    ppermute x19, starting transfers between devices, permute(): return lax.ppermute(array, axis, [(i, i ^ step) for i in range(size)])  23.2 us
    ppermute x19, waiting for transfers between devices, permute(): return lax.ppermute(array, axis, [(i, i ^ step) for i in range(size)])  19.1 us
    pallas_call x14, Pallas kernels, call(): pl.pallas_call(body, out_shape=list(outs), in_specs=[FAR if k in far_ins...  9.06 us
    ppermute x2, starting transfers between devices, across(): return lax.ppermute(block, ('dp', 'expert'), pairs)  1.72 us
  transfers between devices with their start and end apart: 21, of which 13 were waited for; matrix products, arithmetic and copies ran while one was open for 0% of the time, Pallas kernels for 12%

commit v1 on v0

--- a/solution.py
+++ b/solution.py
@@ -91,14 +91,11 @@
         blocks[k][...] = sent[k * slots:(k + 1) * slots]
 
 
-def grads_body(experts, width, *refs):
-    placed, *token_blocks = refs[:experts + 1]
-    sources = refs[experts + 1:experts + 5]
-    gate_up, down, *blocks = refs[experts + 5:-3]
+def grads_body(experts, *refs):
+    placed, sources, (gate_up, down, *blocks) = refs[0], refs[1:5], refs[5:-3]
     weight, out_grad, sems = refs[-3:]
     copies = copy_in(sources, (weight, out_grad, gate_up, down), sems)
-    slots = token_blocks[0].shape[0]
-    partner = lax.axis_index("dp") ^ PARTNER
+    slots = blocks[0].shape[0]
     copies[0].wait()
     column = row_to_column(weight[...])
     copies[1].wait()
@@ -106,17 +103,14 @@
     sent = dot(placed[...], scaled, 1, 0).astype(BF)
     for k in range(experts):
         blocks[k][...] = sent[k * slots:(k + 1) * slots]
-    for k, half in enumerate(blocks[experts:]):
-        columns_for(token_blocks[k], half, partner, width)
-        columns_for(blocks[k], half, partner, width, len(MASKS) * width)
     copies[2].wait()
     copies[3].wait()
 
 
-def columns_for(rows, out, device, width, start=0):
-    for k, mask in enumerate(MASKS):
+def columns_for(rows, out, device, masks, width):
+    for k, mask in enumerate(masks):
         at = pl.multiple_of((device ^ mask) * width, width)
-        out[:, start + k * width:start + (k + 1) * width] = rows[:, pl.ds(at, width)]
+        out[:, k * width:(k + 1) * width] = rows[:, pl.ds(at, width)]
 
 
 def gather(blocks, rows):
@@ -125,23 +119,25 @@
         rows[k * slots:(k + 1) * slots, :] = block[...]
 
 
+def pack_body(blocks, width, *refs):
+    sent, rows = refs[blocks:]
+    gather(refs[:blocks], rows)
+    columns_for(rows, sent, lax.axis_index("dp") ^ UP_PARTNER, UP_MASKS, width)
+
+
 def forward_body(experts, width, *refs):
-    blocks, (gate_up, pre_out, own, send, rows) = refs[:experts], refs[experts:]
+    blocks, (gate_up, pre_out, act, own, send, rows) = refs[:experts], refs[experts:]
     gather(blocks, rows)
     pre = dot(rows[...], gate_up[0], 1, 0)
     pre_out[...] = pre
     hidden = pre.shape[1] // 2
     gate, up = pre[:, :hidden], pre[:, hidden:]
-    send[:, :hidden] = (gate * jax.nn.sigmoid(gate) * up).astype(BF)
-    if width == 0:
-        return
-    device = lax.axis_index("dp")
-    columns_for(rows, own, device, width)
-    late = rows.shape[0] // 2
-    for k, mask in enumerate(MASKS):
-        at = pl.multiple_of((device ^ PARTNER ^ mask) * width, width)
-        to, start = (k // 2) * late, hidden + (k % 2) * width
-        send[to:to + late, start:start + width] = rows[late:, pl.ds(at, width)]
+    act[...] = (gate * jax.nn.sigmoid(gate) * up).astype(BF)
+    if width:
+        device = lax.axis_index("dp")
+        columns_for(rows, own, device, UP_MASKS, width)
+        late = rows.at[rows.shape[0] - send.shape[0]:]
+        columns_for(late, send, device ^ UP_PARTNER, UP_MASKS, width)
 
 
 def backward_body(experts, width, *refs):
@@ -153,17 +149,15 @@
     sig = jax.nn.sigmoid(gate)
     d_gate[...] = (d_act * up * sig * (1.0 + gate * (1.0 - sig))).astype(BF)
     d_up[...] = (d_act * (gate * sig)).astype(BF)
-    if width == 0:
-        return
-    device = lax.axis_index("dp")
-    columns_for(rows, own, device, width)
-    late = rows.shape[0] // 2
-    columns_for(rows.at[late:], send, device ^ PARTNER, width)
-
-
-def return_body(experts, first, d_gate, d_up, gate_up, down, *blocks):
+    if width:
+        device = lax.axis_index("dp")
+        columns_for(rows, own, device, DOWN_MASKS, width)
+        columns_for(rows, send, device ^ DOWN_PARTNER, DOWN_MASKS, width)
+
+
+def return_body(experts, act, d_gate, d_up, gate_up, down, *blocks):
     slots = blocks[0].shape[0] // 2
-    result = dot(first[:, :down.shape[1]], down[0], 1, 0).astype(BF)
+    result = dot(act[...], down[0], 1, 0).astype(BF)
     for k in range(experts):
         blocks[k][:slots] = result[k * slots:(k + 1) * slots]
     hidden = d_gate.shape[1]
@@ -173,22 +167,16 @@
         blocks[k][slots:] = moved[k * slots:(k + 1) * slots]
 
 
-def terms_body(joined, hidden, *refs):
-    halves, (own, factor, factor_in, late, kept, far, near, rows) = refs[:joined], refs[joined:]
-    width, half = kept.shape[0], own.shape[1]
-    slots, cut = halves[0].shape[0], rows.shape[0] // 2
-    start = 0 if hidden else half
-    for k, block in enumerate(halves):
-        rows[k * slots:(k + 1) * slots, :] = block[:, start:start + half]
-    if hidden:
-        rows[cut:, :half // 2] = late[:cut, hidden:]
-        rows[cut:, half // 2:] = late[cut:, hidden:]
-    else:
-        rows[cut:, :] = late[...]
-    columns = kept.shape[1]
-    for k, out in enumerate((kept, near.at[:width], far, near.at[width:])):
+def terms_body(order, pieces, own, factor, *refs):
+    parts, (factor_in, kept, far, near, rows) = refs[:pieces], refs[pieces:]
+    start = 0
+    for part in parts:
+        rows[start:start + part.shape[0], :] = part[...]
+        start += part.shape[0]
+    width = kept.shape[0]
+    for k, out in zip(order, (kept, near.at[:width], far, near.at[width:])):
         at = slice(k * width, (k + 1) * width)
-        total = dot(own[:, at], factor[:, :columns], 0, 0) + dot(rows[:, at], factor_in[:, :columns], 0, 0)
+        total = dot(own[:, at], factor[...], 0, 0) + dot(rows[:, at], factor_in[...], 0, 0)
         out[...] = total.astype(out.dtype)
 
 
@@ -200,23 +188,23 @@
     return kept[...] + near[:kept.shape[0], :].astype(F32) + distant[...].astype(F32)
 
 
-def early_body(*refs):
+def early_body(places, *refs):
     first, second, (out, held, sems) = refs[:3], refs[3:6], refs[6:]
     width = held.shape[2]
     copies = []
     for k, terms in enumerate((first, second)):
         held[k] = total_of(*terms)
-        target = out.at[:, pl.ds(2 * k * width, width)]
+        target = out.at[:, pl.ds(places[k] * width, width)]
         copies.append(pltpu.make_async_copy(held.at[k], target, sems.at[k]))
         copies[k].start()
     for copy in copies:
         copy.wait()
 
 
-def last_body(kept, near, distant, out_in, out, held, sem):
+def last_body(place, kept, near, distant, out_in, out, held, sem):
     held[...] = total_of(kept, near, distant)
     width = held.shape[1]
-    copy = pltpu.make_async_copy(held, out.at[:, pl.ds(width, width)], sem)
+    copy = pltpu.make_async_copy(held, out.at[:, pl.ds(place * width, width)], sem)
     copy.start()
     copy.wait()
 
@@ -242,13 +230,6 @@
 
 def exchange(blocks, axis, size, stride=1):
     return [blocks[0]] + [permute(blocks[k], axis, size, k * stride) for k in range(1, len(blocks))]
-
-
-def across(block, k, experts, shards):
-    pairs = [
-        (i * experts + j, (i ^ PARTNER) * experts + (j ^ k)) for i in range(shards) for j in range(experts)
-    ]
-    return lax.ppermute(block, ("dp", "expert"), pairs)
 
 
 def on_device(tokens, route_ids, route_weight, w_gate_up, w_down, out_grad):
@@ -262,7 +243,7 @@
     rows = experts * slots
     share = width // shards
     staged = is_staged(width, shards)
-    half = len(MASKS) * share if staged else 256
+    half = 4 * share if staged else 128
     ids = route_ids.reshape(1, count)
     weight = route_weight.reshape(1, count)
 
@@ -273,62 +254,68 @@
         [pltpu.VMEM(a.shape, a.dtype) for a in (ids, tokens)] + [pltpu.SemaphoreType.DMA((2,))],
         flops=2 * rows * count * width, far_ins=(0, 1))
     token_blocks = exchange(sent_tokens, "expert", experts)
-    joined = experts // 2 if staged else 0
     gate_up, down, *sent = call(
-        functools.partial(grads_body, experts, share),
-        [shape(w_gate_up.shape, BF), shape(w_down.shape, BF)] + [block] * experts
-        + [shape((slots, 2 * half), BF)] * joined,
-        (placed, *sent_tokens, weight, out_grad, w_gate_up, w_down),
+        functools.partial(grads_body, experts),
+        [shape(w_gate_up.shape, BF), shape(w_down.shape, BF)] + [block] * experts,
+        (placed, weight, out_grad, w_gate_up, w_down),
         [pltpu.VMEM(a.shape, a.dtype) for a in (weight, out_grad)] + [pltpu.SemaphoreType.DMA((4,))],
-        flops=2 * rows * count * width, far_ins=tuple(range(experts + 1, experts + 5)))
+        flops=2 * rows * count * width, far_ins=(1, 2, 3, 4))
     grad_blocks = exchange(sent[:experts], "expert", experts)
     scratch = [pltpu.VMEM((rows, width), BF)]
-    own_shape, late_shape = shape((rows, half), BF), shape((rows // 2, half), BF)
+    side = shape((rows, half), BF)
+    early = experts // 2
+    part = shape((early * slots, half), BF)
     piece = share if staged else 0
-    pre, own_rows, first = call(
+    pre, act, own_rows, sent_rows = call(
         functools.partial(forward_body, experts, piece),
-        [shape((rows, 2 * hidden), F32), own_shape, shape((rows, hidden + half // 2), BF)],
+        [shape((rows, 2 * hidden), F32), shape((rows, hidden), BF), side, part],
         (*token_blocks, gate_up), scratch, flops=4 * rows * hidden * width)
     own_grads, late_grads, d_gate, d_up = call(
         functools.partial(backward_body, experts, piece),
-        [own_shape, late_shape] + [shape((rows, hidden), BF)] * 2,
+        [side, side] + [shape((rows, hidden), BF)] * 2,
         (*grad_blocks, pre, down), scratch, flops=2 * rows * hidden * width)
     back = call(
         functools.partial(return_body, experts), [shape((2 * slots, width), BF)] * experts,
-        (first, d_gate, d_up, gate_up, down), flops=6 * rows * hidden * width)
+        (act, d_gate, d_up, gate_up, down), flops=6 * rows * hidden * width)
     if staged:
-        first_in = permute(first, "dp", shards, PARTNER)
-        both = [across(sent[experts + k], k, experts, shards) for k in range(joined)]
-        late_in = permute(late_grads, "dp", shards, PARTNER)
-        d_gate_in = permute(d_gate, "dp", shards, PARTNER)
-        d_up_in = permute(d_up, "dp", shards, PARTNER)
+        act_in = permute(act, "dp", shards, DOWN_PARTNER)
+        packed, = call(
+            functools.partial(pack_body, early, share), [part], token_blocks[:early],
+            [pltpu.VMEM((early * slots, width), BF)])
+        rows_in = [permute(packed, "dp", shards, UP_PARTNER), permute(sent_rows, "dp", shards, UP_PARTNER)]
+        grads_in = [permute(late_grads, "dp", shards, DOWN_PARTNER)]
+        d_gate_in = permute(d_gate, "dp", shards, UP_PARTNER)
+        d_up_in = permute(d_up, "dp", shards, UP_PARTNER)
         one = shape((share, hidden), F32)
 
-        def summed(start, own, factor, factor_in, late):
+        def summed(own, factor, rows_in, factor_in, masks, order):
             kept, far, near = call(
-                functools.partial(terms_body, joined, start),
-                [one, one, shape((2 * share, hidden), BF)], (*both, own, factor, factor_in, late),
+                functools.partial(terms_body, order, len(rows_in)),
+                [one, one, shape((2 * share, hidden), BF)], (own, factor, *rows_in, factor_in),
                 [pltpu.VMEM((rows, half), BF)], flops=4 * rows * hidden * half)
-            near = permute(near, "dp", shards, MASKS[1])
+            near = permute(near, "dp", shards, masks[order[1]])
             distant, = call(pair_body, [shape((share, hidden), BF)], (far, near))
-            return kept, near, permute(distant, "dp", shards, MASKS[2])
-
-        downs = summed(0, own_grads, first, first_in, late_in)
-        gates = summed(hidden, own_rows, d_gate, d_gate_in, first_in)
-        ups = summed(hidden, own_rows, d_up, d_up_in, first_in)
+            return kept, near, permute(distant, "dp", shards, masks[order[2]])
+
+        gates = summed(own_rows, d_gate, rows_in, d_gate_in, UP_MASKS, GATE_ORDER)
+        downs = summed(own_grads, act, grads_in, act_in, DOWN_MASKS, DOWN_ORDER)
+        ups = summed(own_rows, d_up, rows_in, d_up_in, UP_MASKS, UP_ORDER)
         whole = shape((share, 3 * hidden), F32)
+        terms = [gates, ups, downs]
+        first, second, final = FINISH
         weight_grad, = call(
-            early_body, [whole], (*gates, *downs),
+            functools.partial(early_body, (first, second)), [whole],
+            (*terms[first], *terms[second]),
             [pltpu.VMEM((2, share, hidden), F32), pltpu.SemaphoreType.DMA((2,))], far_outs=(0,))
         weight_grad, = call(
-            last_body, [whole], (*ups, weight_grad),
+            functools.partial(last_body, final), [whole], (*terms[final], weight_grad),
             [pltpu.VMEM((share, hidden), F32), pltpu.SemaphoreType.DMA],
             far_ins=(3,), far_outs=(0,), aliases={3: 0})
     else:
         weight_grad = lax.psum_scatter(
             jnp.concatenate([
                 dot(jnp.concatenate(token_blocks, axis=0), jnp.concatenate([d_gate, d_up], axis=1), 0, 0),
-                dot(jnp.concatenate(grad_blocks, axis=0), first[:, :hidden], 0, 0)], axis=1),
+                dot(jnp.concatenate(grad_blocks, axis=0), act, 0, 0)], axis=1),
             "dp", scatter_dimension=0, tiled=True)
     returned = exchange(back, "expert", experts)
     mixed, token_grad, weight_row = call(
@@ -342,8 +329,11 @@
     return shards == 8 and (width // shards) % 128 == 0
 
 
-PARTNER = 2
-MASKS = (0, 1, 4, 5)
+DOWN_PARTNER, DOWN_MASKS = 1, (0, 2, 4, 6)
+UP_PARTNER, UP_MASKS = 2, (0, 1, 4, 5)
+FINISH = (0, 1, 2)
+GATE_ORDER = (0, 2, 1, 3)
+DOWN_ORDER = UP_ORDER = (0, 1, 2, 3)
 
 
 def solution(mesh):

time: 54.1 us -> 50.5 us (0.933)
  waiting for transfers between devices: 19.2 us -> 15.8 us
    ppermute x19 -> x21, waiting for transfers between devices: 19.1 us -> 15.8 us  [permute(): return lax.ppermute(array, axis, [(i, i ^ step) for i in range(size)])]
    ppermute x2 -> x0, starting transfers between devices: 1.72 us -> none  [across(): return lax.ppermute(block, ('dp', 'expert'), pairs)]
    ppermute x19 -> x21, starting transfers between devices: 23.2 us -> 24.6 us  [permute(): return lax.ppermute(array, axis, [(i, i ^ step) for i in range(size)])]
    pallas_call x14 -> x15, Pallas kernels: 9.06 us -> 9.12 us  [call(): pl.pallas_call(body, out_shape=list(outs), in_specs=[FAR if k in far_ins...]
  transfers between devices with their start and end apart: 21 -> 21, of which waited for: 13 -> 9; matrix products, arithmetic and copies ran while one was open for 0% -> 0% of each run, Pallas kernels for 12% -> 14%
where the time goes in v1:
time: 50.5 us; the launch traced here: 50.4 us
  starting transfers between devices  24.6 us (49%)
  waiting for transfers between devices  15.8 us (31%)
  Pallas kernels  9.12 us (18%)
  between operations  0.78 us (2%)
    ppermute x21, starting transfers between devices, permute(): return lax.ppermute(array, axis, [(i, i ^ step) for i in range(size)])  24.6 us
    ppermute x21, waiting for transfers between devices, permute(): return lax.ppermute(array, axis, [(i, i ^ step) for i in range(size)])  15.8 us
    pallas_call x15, Pallas kernels, call(): pl.pallas_call(body, out_shape=list(outs), in_specs=[FAR if k in far_ins...  9.12 us
  transfers between devices with their start and end apart: 21, of which 9 were waited for; matrix products, arithmetic and copies ran while one was open for 0% of the time, Pallas kernels for 14%

profile of v1, /device:TPU:0, one launch (start us, length us, event | category | flops | bytes accessed | tf_op | source)
XLA Modules:
  0.0 50.4 jit_solution(7770541128175054821)
XLA Ops:
  0.6 1.2 %shard_map.93 = (bf16[192,128]{1,0:T(8,128)(2,1)S(1)}, bf16[48,1024]{1,0:T(8,128)(2,1)S(1)}, bf16[48,1024]{1,0:T(8,128)(2,1)S(1)}, bf16[48,1024]{1,0:T(8,128)(2,1)S(1)}, bf16[48,1024]{1,0:T(8,128)(2,1)S(1)}) custom-call(s32[1,128]{1,0:T(1,128)} %bitcast.7, bf16[128,1024]{1,0:T(8,128)(2,1)} %tokens_in.1), custom_call_target="tpu_custom_call" | custom-call | flops 50331648 | bytes 705024 | tf_op jit(solution)/shard_map/pallas_call | solution.py:27
  1.9 0.6 %collective-permute-start = (bf16[48,1024]{1,0:T(8,128)(2,1)S(1)}, bf16[48,1024]{1,0:T(8,128)(2,1)S(1)}, u32[]{:S(2)}, u32[]{:S(2)}) collective-permute-start(bf16[48,1024]{1,0:T(8,128)(2,1)S(1)} %get-tuple-element.40), channel_id=1, source_target_pairs={{0,1},{1,0},{2,3},{3,2},{4,5},{5,4},{6,7},{7,6},{8,9},{9,8},{10,11... | collective-permute-start | bytes 294920 | tf_op jit(solution)/shard_map/ppermute | solution.py:228
  2.4 2.6 %collective-permute-start.1 = (bf16[48,1024]{1,0:T(8,128)(2,1)S(1)}, bf16[48,1024]{1,0:T(8,128)(2,1)S(1)}, u32[]{:S(2)}, u32[]{:S(2)}) collective-permute-start(bf16[48,1024]{1,0:T(8,128)(2,1)S(1)} %get-tuple-element.41), channel_id=1, source_target_pairs={{0,2},{1,3},{2,0},{3,1},{4,6},{5,7},{6,4},{7,5},{8,10},{9,11},{10,... | collective-permute-start | bytes 294920 | tf_op jit(solution)/shard_map/ppermute | solution.py:228
  5.0 0.0 collective-permute-start.2
  5.0 1.7 %shard_map.94 = (bf16[1,1024,768]{2,1,0:T(8,128)(2,1)S(1)}, bf16[1,384,1024]{2,1,0:T(8,128)(2,1)S(1)}, bf16[48,1024]{1,0:T(8,128)(2,1)S(1)}, bf16[48,1024]{1,0:T...) custom-call(bf16[192,128]{1,0:T(8,128)(2,1)S(1)} %get-tuple-element.43.refs_0_.refs_4_, ...), custom_call_target="tpu_custom_call" | custom-call | flops 50331648 | bytes 5423616 | tf_op jit(solution)/shard_map/pallas_call | solution.py:27
  6.8 0.2 collective-permute-start.3
  7.0 1.9 %collective-permute-start.4 = (bf16[48,1024]{1,0:T(8,128)(2,1)S(1)}, bf16[48,1024]{1,0:T(8,128)(2,1)S(1)}, u32[]{:S(2)}, u32[]{:S(2)}) collective-permute-start(bf16[48,1024]{1,0:T(8,128)(2,1)S(1)} %get-tuple-element.48), channel_id=1, source_target_pairs={{0,2},{1,3},{2,0},{3,1},{4,6},{5,7},{6,4},{7,5},{8,10},{9,11},{10,... | collective-permute-start | bytes 294920 | tf_op jit(solution)/shard_map/ppermute | solution.py:228
  8.9 0.0 collective-permute-done.refs_1_
  8.9 0.0 collective-permute-start.5
  9.0 0.0 collective-permute-done.1.refs_2_
  9.0 1.7 %collective-permute-start.13 = (bf16[96,512]{1,0:T(8,128)(2,1)S(1)}, bf16[96,512]{1,0:T(8,128)(2,1)S(1)}, u32[]{:S(2)}, u32[]{:S(2)}) collective-permute-start(bf16[96,512]{1,0:T(8,128)(2,1)S(1)} %shard_map.101), channel_id=1, source_target_pairs={{0,8},{4,12},{8,0},{12,4},{16,24},{20,28},{24,16},{28,20},{1,9},{5... | collective-permute-start | bytes 294920 | tf_op jit(solution)/shard_map/ppermute | solution.py:228
  10.7 0.0 collective-permute-done.2.refs_3_
  10.8 0.5 %shard_map.95 = (f32[192,768]{1,0:T(8,128)S(1)}, bf16[192,384]{1,0:T(8,128)(2,1)S(1)}, bf16[192,512]{1,0:T(8,128)(2,1)S(1)}, bf16[96,512]{1,0:T(8,128)(2,1)S(1)}) custom-call(bf16[48,1024]{1,0:T(8,128)(2,1)S(1)} %get-tuple-element.39.refs_0_, bf16[48,1024]{1,0:T(8,128)(2,1)S(1)} %collective-permute-done.refs_1_, ...), custom_call_target="tpu_custom_call" | custom-call | flops 301989888 | bytes 2998272 | tf_op jit(solution)/shard_map/pallas_call | solution.py:27
  11.3 0.0 collective-permute-done.3.refs_1_
  11.3 1.5 %collective-permute-done.4.refs_2_ = bf16[48,1024]{1,0:T(8,128)(2,1)S(1)} collective-permute-done((bf16[48,1024]{1,0:T(8,128)(2,1)S(1)}, bf16[48,1024]{1,0:T(8,128)(2,1)S(1)}, u32[]{:S(2)}, u32[]{:S(2)}) %collective-permute-start.4) | collective-permute-done | bytes 98336 | tf_op jit(solution)/shard_map/ppermute | solution.py:228
  12.9 1.6 %collective-permute-done.5.refs_3_ = bf16[48,1024]{1,0:T(8,128)(2,1)S(1)} collective-permute-done((bf16[48,1024]{1,0:T(8,128)(2,1)S(1)}, bf16[48,1024]{1,0:T(8,128)(2,1)S(1)}, u32[]{:S(2)}, u32[]{:S(2)}) %collective-permute-start.5) | collective-permute-done | bytes 98336 | tf_op jit(solution)/shard_map/ppermute | solution.py:228
  14.4 0.5 %shard_map.96 = (bf16[192,512]{1,0:T(8,128)(2,1)S(1)}, bf16[192,512]{1,0:T(8,128)(2,1)S(1)}, bf16[192,384]{1,0:T(8,128)(2,1)S(1)}, bf16[192,384]{1,0:T(8,128)(2,1)S(1)}) custom-call(bf16[48,1024]{1,0:T(8,128)(2,1)S(1)} %get-tuple-element.46.refs_0_, bf16[48,1024]{1,0:T(8,128)(2,1)S(1)} %collective-permute-done.3.refs_1_, ...), custom_call_target="tpu_custom_call" | custom-call | flops 150994944 | bytes 2457600 | tf_op jit(solution)/shard_map/pallas_call | solution.py:27
  15.0 1.6 %collective-permute-start.18 = (bf16[192,384]{1,0:T(8,128)(2,1)S(1)}, bf16[192,384]{1,0:T(8,128)(2,1)S(1)}, u32[]{:S(2)}, u32[]{:S(2)}) collective-permute-start(bf16[192,384]{1,0:T(8,128)(2,1)S(1)} %get-tuple-element.53.d_up.factor), channel_id=1, source_target_pairs={{0,8},{4,12},{8,0},{12,4},{16,24},{20,28},{24,16},{28,20},{1,9},{5... | collective-permute-start | bytes 442376 | tf_op jit(solution)/shard_map/ppermute | solution.py:228
  16.6 1.5 %collective-permute-start.9 = (bf16[192,512]{1,0:T(8,128)(2,1)S(1)}, bf16[192,512]{1,0:T(8,128)(2,1)S(1)}, u32[]{:S(2)}, u32[]{:S(2)}) collective-permute-start(bf16[192,512]{1,0:T(8,128)(2,1)S(1)} %get-tuple-element.62), channel_id=1, source_target_pairs={{0,4},{4,0},{8,12},{12,8},{16,20},{20,16},{24,28},{28,24},{1,5},{5... | collective-permute-start | bytes 589832 | tf_op jit(solution)/shard_map/ppermute | solution.py:228
  18.1 0.4 collective-permute-start.14
  18.6 1.6 %collective-permute-start.15 = (bf16[192,384]{1,0:T(8,128)(2,1)S(1)}, bf16[192,384]{1,0:T(8,128)(2,1)S(1)}, u32[]{:S(2)}, u32[]{:S(2)}) collective-permute-start(bf16[192,384]{1,0:T(8,128)(2,1)S(1)} %get-tuple-element.52.d_gate.factor), channel_id=1, source_target_pairs={{0,8},{4,12},{8,0},{12,4},{16,24},{20,28},{24,16},{28,20},{1,9},{5... | collective-permute-start | bytes 442376 | tf_op jit(solution)/shard_map/ppermute | solution.py:228
  20.1 0.0 collective-permute-done.13.refs_0_
  20.1 0.5 collective-permute-start.10
  20.6 3.1 %collective-permute-done.14.refs_1_ = bf16[96,512]{1,0:T(8,128)(2,1)S(1)} collective-permute-done((bf16[96,512]{1,0:T(8,128)(2,1)S(1)}, bf16[96,512]{1,0:T(8,128)(2,1)S(1)}, u32[]{:S(2)}, u32[]{:S(2)}) %collective-permute-start.14) | collective-permute-done | bytes 98336 | tf_op jit(solution)/shard_map/ppermute | solution.py:228
  23.8 0.5 shard_map.104
  24.3 1.6 %collective-permute-start.19 = (bf16[256,384]{1,0:T(8,128)(2,1)S(1)}, bf16[256,384]{1,0:T(8,128)(2,1)S(1)}, u32[]{:S(2)}, u32[]{:S(2)}) collective-permute-start(bf16[256,384]{1,0:T(8,128)(2,1)S(1)} %get-tuple-element.72), channel_id=1, source_target_pairs={{0,4},{4,0},{8,12},{12,8},{16,20},{20,16},{24,28},{28,24},{1,5},{5... | collective-permute-start | bytes 589832 | tf_op jit(solution)/shard_map/ppermute | solution.py:228
  25.9 0.3 collective-permute-done.15.refs_2_
  26.2 0.5 shard_map.102
  26.7 2.8 %collective-permute-start.16 = (bf16[256,384]{1,0:T(8,128)(2,1)S(1)}, bf16[256,384]{1,0:T(8,128)(2,1)S(1)}, u32[]{:S(2)}, u32[]{:S(2)}) collective-permute-start(bf16[256,384]{1,0:T(8,128)(2,1)S(1)} %get-tuple-element.69), channel_id=1, source_target_pairs={{0,16},{4,20},{8,24},{12,28},{16,0},{20,4},{24,8},{28,12},{1,17},{... | collective-permute-start | bytes 589832 | tf_op jit(solution)/shard_map/ppermute | solution.py:228
  29.5 0.5 shard_map.99
  30.0 0.0 copy-start
  30.0 0.0 copy-start.1
  30.1 1.6 %collective-permute-start.11 = (bf16[256,384]{1,0:T(8,128)(2,1)S(1)}, bf16[256,384]{1,0:T(8,128)(2,1)S(1)}, u32[]{:S(2)}, u32[]{:S(2)}) collective-permute-start(bf16[256,384]{1,0:T(8,128)(2,1)S(1)} %get-tuple-element.64), channel_id=1, source_target_pairs={{0,8},{4,12},{8,0},{12,4},{16,24},{20,28},{24,16},{28,20},{1,9},{5... | collective-permute-start | bytes 589832 | tf_op jit(solution)/shard_map/ppermute | solution.py:228
  31.7 0.9 %shard_map.97 = (bf16[96,1024]{1,0:T(8,128)(2,1)S(1)}, bf16[96,1024]{1,0:T(8,128)(2,1)S(1)}, bf16[96,1024]{1,0:T(8,128)(2,1)S(1)}, bf16[96,1024]{1,0:T(8,128)(2,1)S(1)}) custom-call(bf16[192,384]{1,0:T(8,128)(2,1)S(1)} %get-tuple-element.45.act.factor, bf16[192,384]{1,0:T(8,128)(2,1)S(1)} %get-tuple-element.52.d_gate.factor, ...), custom_call_target="tpu_custom_call" | custom-call | flops 452984832 | bytes 3588096 | tf_op jit(solution)/shard_map/pallas_call | solution.py:27
  32.6 0.1 collective-permute-start.6
  32.7 1.6 %collective-permute-start.7 = (bf16[96,1024]{1,0:T(8,128)(2,1)S(1)}, bf16[96,1024]{1,0:T(8,128)(2,1)S(1)}, u32[]{:S(2)}, u32[]{:S(2)}) collective-permute-start(bf16[96,1024]{1,0:T(8,128)(2,1)S(1)} %get-tuple-element.56), channel_id=1, source_target_pairs={{0,2},{1,3},{2,0},{3,1},{4,6},{5,7},{6,4},{7,5},{8,10},{9,11},{10,... | collective-permute-start | bytes 589832 | tf_op jit(solution)/shard_map/ppermute | solution.py:228
  34.2 0.3 collective-permute-start.8
  34.5 3.9 %collective-permute-done.16.arrived.refs_1_ = bf16[256,384]{1,0:T(8,128)(2,1)S(1)} collective-permute-done((bf16[256,384]{1,0:T(8,128)(2,1)S(1)}, bf16[256,384]{1,0:T(8,128)(2,1)S(1)}, u32[]{:S(2)}, u32[]{:S(2)}) %collective-permute-start.16) | collective-permute-done | bytes 196640 | tf_op jit(solution)/shard_map/ppermute | solution.py:228
  38.4 0.0 collective-permute-start.20
  38.5 0.7 %collective-permute-done.11.arrived.near = bf16[256,384]{1,0:T(8,128)(2,1)S(1)} collective-permute-done((bf16[256,384]{1,0:T(8,128)(2,1)S(1)}, bf16[256,384]{1,0:T(8,128)(2,1)S(1)}, u32[]{:S(2)}, u32[]{:S(2)}) %collective-permute-start.11) | collective-permute-done | bytes 196640 | tf_op jit(solution)/shard_map/ppermute | solution.py:228
  39.2 1.6 %collective-permute-start.17 = (bf16[128,384]{1,0:T(8,128)(2,1)S(1)}, bf16[128,384]{1,0:T(8,128)(2,1)S(1)}, u32[]{:S(2)}, u32[]{:S(2)}) collective-permute-start(bf16[128,384]{1,0:T(8,128)(2,1)S(1)} %shard_map.103), channel_id=1, source_target_pairs={{0,4},{4,0},{8,12},{12,8},{16,20},{20,16},{24,28},{28,24},{1,5},{5... | collective-permute-start | bytes 294920 | tf_op jit(solution)/shard_map/ppermute | solution.py:228
  40.8 2.3 %collective-permute-start.12 = (bf16[128,384]{1,0:T(8,128)(2,1)S(1)}, bf16[128,384]{1,0:T(8,128)(2,1)S(1)}, u32[]{:S(2)}, u32[]{:S(2)}) collective-permute-start(bf16[128,384]{1,0:T(8,128)(2,1)S(1)} %shard_map.100), channel_id=1, source_target_pairs={{0,16},{4,20},{8,24},{12,28},{16,0},{20,4},{24,8},{28,12},{1,17},{... | collective-permute-start | bytes 294920 | tf_op jit(solution)/shard_map/ppermute | solution.py:228
  43.1 0.5 %collective-permute-done.8.refs_3_ = bf16[96,1024]{1,0:T(8,128)(2,1)S(1)} collective-permute-done((bf16[96,1024]{1,0:T(8,128)(2,1)S(1)}, bf16[96,1024]{1,0:T(8,128)(2,1)S(1)}, u32[]{:S(2)}, u32[]{:S(2)}) %collective-permute-start.8) | collective-permute-done | bytes 196640 | tf_op jit(solution)/shard_map/ppermute | solution.py:228
  43.6 1.1 %shard_map.98 = (bf16[128,1024]{1,0:T(8,128)(2,1)}, bf16[128,1024]{1,0:T(8,128)(2,1)}, f32[1,128]{1,0:T(1,128)}) custom-call(bf16[96,1024]{1,0:T(8,128)(2,1)S(1)} %get-tuple-element.54.refs_0_, bf16[96,1024]{1,0:T(8,128)(2,1)S(1)} %collective-permute-done.6.refs_1_, bf16[96,1024]{1,0:T(8,128)(2,1)S(1)} %collective-permute-done.7.refs_2_, ...), custom_call_target="tpu_custom_call" | custom-call | flops 100663296 | bytes 1623040 | tf_op jit(solution)/shard_map/pallas_call | solution.py:27
  44.8 1.7 %collective-permute-done.20.refs_5_ = bf16[128,384]{1,0:T(8,128)(2,1)S(1)} collective-permute-done((bf16[128,384]{1,0:T(8,128)(2,1)S(1)}, bf16[128,384]{1,0:T(8,128)(2,1)S(1)}, u32[]{:S(2)}, u32[]{:S(2)}) %collective-permute-start.20) | collective-permute-done | bytes 98336 | tf_op jit(solution)/shard_map/ppermute | solution.py:228
  46.5 0.8 %shard_map.106.out_in = f32[128,1152]{1,0:T(8,128)} custom-call(f32[128,384]{1,0:T(8,128)S(1)} %get-tuple-element.68.refs_0_, bf16[256,384]{1,0:T(8,128)(2,1)S(1)} %collective-permute-done.16.arrived.refs_1_, bf16[128,384]{1,0:T(8,128)(2,1)S(1)} %collective-permute-done.17.refs_2_, f32[128,384]{1,0:T(8,128)S(1)} %get-tuple-element.71.refs_3_, ...), custom_call_target="tpu_custom_call" | custom-call | bytes 1572864 | tf_op jit(solution)/shard_map/pallas_call | solution.py:27
  47.3 2.4 %collective-permute-done.12.distant = bf16[128,384]{1,0:T(8,128)(2,1)S(1)} collective-permute-done((bf16[128,384]{1,0:T(8,128)(2,1)S(1)}, bf16[128,384]{1,0:T(8,128)(2,1)S(1)}, u32[]{:S(2)}, u32[]{:S(2)}) %collective-permute-start.12) | collective-permute-done | bytes 98336 | tf_op jit(solution)/shard_map/ppermute | solution.py:228
  49.7 0.7 %shard_map.107 = f32[128,1152]{1,0:T(8,128)} custom-call(f32[128,384]{1,0:T(8,128)S(1)} %get-tuple-element.63.kept, bf16[256,384]{1,0:T(8,128)(2,1)S(1)} %collective-permute-done.11.arrived.near, bf16[128,384]{1,0:T(8,128)(2,1)S(1)} %collective-permute-done.12.distant, f32[128,1152]{1,0:T(8,128)} %shard_map.106.out_in), custom_call_target="tpu_custom_call", output_to_operand_aliasing={{}: (3, {})} | custom-call | bytes 1671168 | tf_op jit(solution)/shard_map/pallas_call | solution.py:27
  (13 shorter events, 0.1 us)
Async XLA Ops:
  1.9 7.1 %collective-permute-start = (bf16[48,1024]{1,0:T(8,128)(2,1)S(1)}, bf16[48,1024]{1,0:T(8,128)(2,1)S(1)}, u32[]{:S(2)}, u32[]{:S(2)}) collective-permute-start(bf16[48,1024]{1,0:T(8,128)(2,1)S(1)} %get-tuple-element.40), channel_id=1, source_target_pairs={{0,1},{1,0},{2,3},{3,2},{4,5},{5,4},{6,7},{7,6},{8,9},{9,8},{10,11... | collective-permute-start | bytes 294920 | tf_op jit(solution)/shard_map/ppermute | solution.py:228
  2.4 6.6 %collective-permute-start.1 = (bf16[48,1024]{1,0:T(8,128)(2,1)S(1)}, bf16[48,1024]{1,0:T(8,128)(2,1)S(1)}, u32[]{:S(2)}, u32[]{:S(2)}) collective-permute-start(bf16[48,1024]{1,0:T(8,128)(2,1)S(1)} %get-tuple-element.41), channel_id=1, source_target_pairs={{0,2},{1,3},{2,0},{3,1},{4,6},{5,7},{6,4},{7,5},{8,10},{9,11},{10,... | collective-permute-start | bytes 294920 | tf_op jit(solution)/shard_map/ppermute | solution.py:228
  5.0 5.8 %collective-permute-start.2 = (bf16[48,1024]{1,0:T(8,128)(2,1)S(1)}, bf16[48,1024]{1,0:T(8,128)(2,1)S(1)}, u32[]{:S(2)}, u32[]{:S(2)}) collective-permute-start(bf16[48,1024]{1,0:T(8,128)(2,1)S(1)} %get-tuple-element.42), channel_id=1, source_target_pairs={{0,3},{1,2},{2,1},{3,0},{4,7},{5,6},{6,5},{7,4},{8,11},{9,10},{10,... | collective-permute-start | bytes 294920 | tf_op jit(solution)/shard_map/ppermute | solution.py:228
  6.8 4.5 %collective-permute-start.3 = (bf16[48,1024]{1,0:T(8,128)(2,1)S(1)}, bf16[48,1024]{1,0:T(8,128)(2,1)S(1)}, u32[]{:S(2)}, u32[]{:S(2)}) collective-permute-start(bf16[48,1024]{1,0:T(8,128)(2,1)S(1)} %get-tuple-element.47), channel_id=1, source_target_pairs={{0,1},{1,0},{2,3},{3,2},{4,5},{5,4},{6,7},{7,6},{8,9},{9,8},{10,11... | collective-permute-start | bytes 294920 | tf_op jit(solution)/shard_map/ppermute | solution.py:228
  7.0 5.9 %collective-permute-start.4 = (bf16[48,1024]{1,0:T(8,128)(2,1)S(1)}, bf16[48,1024]{1,0:T(8,128)(2,1)S(1)}, u32[]{:S(2)}, u32[]{:S(2)}) collective-permute-start(bf16[48,1024]{1,0:T(8,128)(2,1)S(1)} %get-tuple-element.48), channel_id=1, source_target_pairs={{0,2},{1,3},{2,0},{3,1},{4,6},{5,7},{6,4},{7,5},{8,10},{9,11},{10,... | collective-permute-start | bytes 294920 | tf_op jit(solution)/shard_map/ppermute | solution.py:228
  8.9 5.5 %collective-permute-start.5 = (bf16[48,1024]{1,0:T(8,128)(2,1)S(1)}, bf16[48,1024]{1,0:T(8,128)(2,1)S(1)}, u32[]{:S(2)}, u32[]{:S(2)}) collective-permute-start(bf16[48,1024]{1,0:T(8,128)(2,1)S(1)} %get-tuple-element.49), channel_id=1, source_target_pairs={{0,3},{1,2},{2,1},{3,0},{4,7},{5,6},{6,5},{7,4},{8,11},{9,10},{10,... | collective-permute-start | bytes 294920 | tf_op jit(solution)/shard_map/ppermute | solution.py:228
  9.0 11.1 %collective-permute-start.13 = (bf16[96,512]{1,0:T(8,128)(2,1)S(1)}, bf16[96,512]{1,0:T(8,128)(2,1)S(1)}, u32[]{:S(2)}, u32[]{:S(2)}) collective-permute-start(bf16[96,512]{1,0:T(8,128)(2,1)S(1)} %shard_map.101), channel_id=1, source_target_pairs={{0,8},{4,12},{8,0},{12,4},{16,24},{20,28},{24,16},{28,20},{1,9},{5... | collective-permute-start | bytes 294920 | tf_op jit(solution)/shard_map/ppermute | solution.py:228
  15.0 8.8 %collective-permute-start.18 = (bf16[192,384]{1,0:T(8,128)(2,1)S(1)}, bf16[192,384]{1,0:T(8,128)(2,1)S(1)}, u32[]{:S(2)}, u32[]{:S(2)}) collective-permute-start(bf16[192,384]{1,0:T(8,128)(2,1)S(1)} %get-tuple-element.53.d_up.factor), channel_id=1, source_target_pairs={{0,8},{4,12},{8,0},{12,4},{16,24},{20,28},{24,16},{28,20},{1,9},{5... | collective-permute-start | bytes 442376 | tf_op jit(solution)/shard_map/ppermute | solution.py:228
  16.6 13.0 %collective-permute-start.9 = (bf16[192,512]{1,0:T(8,128)(2,1)S(1)}, bf16[192,512]{1,0:T(8,128)(2,1)S(1)}, u32[]{:S(2)}, u32[]{:S(2)}) collective-permute-start(bf16[192,512]{1,0:T(8,128)(2,1)S(1)} %get-tuple-element.62), channel_id=1, source_target_pairs={{0,4},{4,0},{8,12},{12,8},{16,20},{20,16},{24,28},{28,24},{1,5},{5... | collective-permute-start | bytes 589832 | tf_op jit(solution)/shard_map/ppermute | solution.py:228
  18.1 5.7 %collective-permute-start.14 = (bf16[96,512]{1,0:T(8,128)(2,1)S(1)}, bf16[96,512]{1,0:T(8,128)(2,1)S(1)}, u32[]{:S(2)}, u32[]{:S(2)}) collective-permute-start(bf16[96,512]{1,0:T(8,128)(2,1)S(1)} %get-tuple-element.67), channel_id=1, source_target_pairs={{0,8},{4,12},{8,0},{12,4},{16,24},{20,28},{24,16},{28,20},{1,9},{5... | collective-permute-start | bytes 294920 | tf_op jit(solution)/shard_map/ppermute | solution.py:228
  18.6 7.7 %collective-permute-start.15 = (bf16[192,384]{1,0:T(8,128)(2,1)S(1)}, bf16[192,384]{1,0:T(8,128)(2,1)S(1)}, u32[]{:S(2)}, u32[]{:S(2)}) collective-permute-start(bf16[192,384]{1,0:T(8,128)(2,1)S(1)} %get-tuple-element.52.d_gate.factor), channel_id=1, source_target_pairs={{0,8},{4,12},{8,0},{12,4},{16,24},{20,28},{24,16},{28,20},{1,9},{5... | collective-permute-start | bytes 442376 | tf_op jit(solution)/shard_map/ppermute | solution.py:228
  20.1 9.4 %collective-permute-start.10 = (bf16[192,384]{1,0:T(8,128)(2,1)S(1)}, bf16[192,384]{1,0:T(8,128)(2,1)S(1)}, u32[]{:S(2)}, u32[]{:S(2)}) collective-permute-start(bf16[192,384]{1,0:T(8,128)(2,1)S(1)} %get-tuple-element.45.act.factor), channel_id=1, source_target_pairs={{0,4},{4,0},{8,12},{12,8},{16,20},{20,16},{24,28},{28,24},{1,5},{5... | collective-permute-start | bytes 442376 | tf_op jit(solution)/shard_map/ppermute | solution.py:228
  24.3 10.0 %collective-permute-start.19 = (bf16[256,384]{1,0:T(8,128)(2,1)S(1)}, bf16[256,384]{1,0:T(8,128)(2,1)S(1)}, u32[]{:S(2)}, u32[]{:S(2)}) collective-permute-start(bf16[256,384]{1,0:T(8,128)(2,1)S(1)} %get-tuple-element.72), channel_id=1, source_target_pairs={{0,4},{4,0},{8,12},{12,8},{16,20},{20,16},{24,28},{28,24},{1,5},{5... | collective-permute-start | bytes 589832 | tf_op jit(solution)/shard_map/ppermute | solution.py:228
  26.7 11.7 %collective-permute-start.16 = (bf16[256,384]{1,0:T(8,128)(2,1)S(1)}, bf16[256,384]{1,0:T(8,128)(2,1)S(1)}, u32[]{:S(2)}, u32[]{:S(2)}) collective-permute-start(bf16[256,384]{1,0:T(8,128)(2,1)S(1)} %get-tuple-element.69), channel_id=1, source_target_pairs={{0,16},{4,20},{8,24},{12,28},{16,0},{20,4},{24,8},{28,12},{1,17},{... | collective-permute-start | bytes 589832 | tf_op jit(solution)/shard_map/ppermute | solution.py:228
  30.0 13.6 %copy-start = (bf16[128,1024]{1,0:T(8,128)(2,1)S(1)}, bf16[128,1024]{1,0:T(8,128)(2,1)}, u32[]{:S(2)}) copy-start(bf16[128,1024]{1,0:T(8,128)(2,1)} %refs_6_.1) | copy-start | bytes 786436
  30.0 13.6 %copy-start.1 = (f32[128,1]{0,1:T(1,128)S(1)}, f32[128,1]{0,1:T(1,128)}, u32[]{:S(2)}) copy-start(f32[128,1]{0,1:T(1,128)} %param.8) | copy-start | bytes 1540
  30.1 9.1 %collective-permute-start.11 = (bf16[256,384]{1,0:T(8,128)(2,1)S(1)}, bf16[256,384]{1,0:T(8,128)(2,1)S(1)}, u32[]{:S(2)}, u32[]{:S(2)}) collective-permute-start(bf16[256,384]{1,0:T(8,128)(2,1)S(1)} %get-tuple-element.64), channel_id=1, source_target_pairs={{0,8},{4,12},{8,0},{12,4},{16,24},{20,28},{24,16},{28,20},{1,9},{5... | collective-permute-start | bytes 589832 | tf_op jit(solution)/shard_map/ppermute | solution.py:228
  32.6 8.2 %collective-permute-start.6 = (bf16[96,1024]{1,0:T(8,128)(2,1)S(1)}, bf16[96,1024]{1,0:T(8,128)(2,1)S(1)}, u32[]{:S(2)}, u32[]{:S(2)}) collective-permute-start(bf16[96,1024]{1,0:T(8,128)(2,1)S(1)} %get-tuple-element.55), channel_id=1, source_target_pairs={{0,1},{1,0},{2,3},{3,2},{4,5},{5,4},{6,7},{7,6},{8,9},{9,8},{10,11... | collective-permute-start | bytes 589832 | tf_op jit(solution)/shard_map/ppermute | solution.py:228
  32.7 10.4 %collective-permute-start.7 = (bf16[96,1024]{1,0:T(8,128)(2,1)S(1)}, bf16[96,1024]{1,0:T(8,128)(2,1)S(1)}, u32[]{:S(2)}, u32[]{:S(2)}) collective-permute-start(bf16[96,1024]{1,0:T(8,128)(2,1)S(1)} %get-tuple-element.56), channel_id=1, source_target_pairs={{0,2},{1,3},{2,0},{3,1},{4,6},{5,7},{6,4},{7,5},{8,10},{9,11},{10,... | collective-permute-start | bytes 589832 | tf_op jit(solution)/shard_map/ppermute | solution.py:228
  34.2 9.4 %collective-permute-start.8 = (bf16[96,1024]{1,0:T(8,128)(2,1)S(1)}, bf16[96,1024]{1,0:T(8,128)(2,1)S(1)}, u32[]{:S(2)}, u32[]{:S(2)}) collective-permute-start(bf16[96,1024]{1,0:T(8,128)(2,1)S(1)} %get-tuple-element.57), channel_id=1, source_target_pairs={{0,3},{1,2},{2,1},{3,0},{4,7},{5,6},{6,5},{7,4},{8,11},{9,10},{10,... | collective-permute-start | bytes 589832 | tf_op jit(solution)/shard_map/ppermute | solution.py:228
  38.4 8.1 %collective-permute-start.20 = (bf16[128,384]{1,0:T(8,128)(2,1)S(1)}, bf16[128,384]{1,0:T(8,128)(2,1)S(1)}, u32[]{:S(2)}, u32[]{:S(2)}) collective-permute-start(bf16[128,384]{1,0:T(8,128)(2,1)S(1)} %shard_map.105), channel_id=1, source_target_pairs={{0,16},{4,20},{8,24},{12,28},{16,0},{20,4},{24,8},{28,12},{1,17},{... | collective-permute-start | bytes 294920 | tf_op jit(solution)/shard_map/ppermute | solution.py:228
  39.2 7.3 %collective-permute-start.17 = (bf16[128,384]{1,0:T(8,128)(2,1)S(1)}, bf16[128,384]{1,0:T(8,128)(2,1)S(1)}, u32[]{:S(2)}, u32[]{:S(2)}) collective-permute-start(bf16[128,384]{1,0:T(8,128)(2,1)S(1)} %shard_map.103), channel_id=1, source_target_pairs={{0,4},{4,0},{8,12},{12,8},{16,20},{20,16},{24,28},{28,24},{1,5},{5... | collective-permute-start | bytes 294920 | tf_op jit(solution)/shard_map/ppermute | solution.py:228
  40.8 8.9 %collective-permute-start.12 = (bf16[128,384]{1,0:T(8,128)(2,1)S(1)}, bf16[128,384]{1,0:T(8,128)(2,1)S(1)}, u32[]{:S(2)}, u32[]{:S(2)}) collective-permute-start(bf16[128,384]{1,0:T(8,128)(2,1)S(1)} %shard_map.100), channel_id=1, source_target_pairs={{0,16},{4,20},{8,24},{12,28},{16,0},{20,4},{24,8},{28,12},{1,17},{... | collective-permute-start | bytes 294920 | tf_op jit(solution)/shard_map/ppermute | solution.py:228

commit v2 on v1

--- a/solution.py
+++ b/solution.py
@@ -119,12 +119,6 @@
         rows[k * slots:(k + 1) * slots, :] = block[...]
 
 
-def pack_body(blocks, width, *refs):
-    sent, rows = refs[blocks:]
-    gather(refs[:blocks], rows)
-    columns_for(rows, sent, lax.axis_index("dp") ^ UP_PARTNER, UP_MASKS, width)
-
-
 def forward_body(experts, width, *refs):
     blocks, (gate_up, pre_out, act, own, send, rows) = refs[:experts], refs[experts:]
     gather(blocks, rows)
@@ -136,18 +130,19 @@
     if width:
         device = lax.axis_index("dp")
         columns_for(rows, own, device, UP_MASKS, width)
-        late = rows.at[rows.shape[0] - send.shape[0]:]
-        columns_for(late, send, device ^ UP_PARTNER, UP_MASKS, width)
+        columns_for(rows, send, device ^ UP_PARTNER, UP_MASKS, width)
 
 
 def backward_body(experts, width, *refs):
-    blocks, (pre, down, own, send, d_gate, d_up, rows) = refs[:experts], refs[experts:]
+    blocks, (pre, down, own, send, d_first, d_gate, d_up, rows) = refs[:experts], refs[experts:]
     gather(blocks, rows)
     d_act = dot(rows[...], down[0], 1, 1)
     hidden = d_act.shape[1]
     gate, up = pre[:, :hidden], pre[:, hidden:]
     sig = jax.nn.sigmoid(gate)
-    d_gate[...] = (d_act * up * sig * (1.0 + gate * (1.0 - sig))).astype(BF)
+    both = (d_act * up * sig * (1.0 + gate * (1.0 - sig))).astype(BF)
+    d_first[...] = both[:, :FIRST]
+    d_gate[...] = both[:, FIRST:]
     d_up[...] = (d_act * (gate * sig)).astype(BF)
     if width:
         device = lax.axis_index("dp")
@@ -155,56 +150,55 @@
         columns_for(rows, send, device ^ DOWN_PARTNER, DOWN_MASKS, width)
 
 
-def return_body(experts, act, d_gate, d_up, gate_up, down, *blocks):
+def return_body(experts, act, d_first, d_gate, d_up, gate_up, down, *blocks):
     slots = blocks[0].shape[0] // 2
     result = dot(act[...], down[0], 1, 0).astype(BF)
     for k in range(experts):
         blocks[k][:slots] = result[k * slots:(k + 1) * slots]
-    hidden = d_gate.shape[1]
-    moved = dot(d_gate[...], gate_up[0, :, :hidden], 1, 1)
+    hidden = d_up.shape[1]
+    moved = dot(d_first[...], gate_up[0, :, :FIRST], 1, 1)
+    moved += dot(d_gate[...], gate_up[0, :, FIRST:hidden], 1, 1)
     moved = (moved + dot(d_up[...], gate_up[0, :, hidden:], 1, 1)).astype(BF)
     for k in range(experts):
         blocks[k][slots:] = moved[k * slots:(k + 1) * slots]
 
 
-def terms_body(order, pieces, own, factor, *refs):
-    parts, (factor_in, kept, far, near, rows) = refs[:pieces], refs[pieces:]
-    start = 0
-    for part in parts:
-        rows[start:start + part.shape[0], :] = part[...]
-        start += part.shape[0]
+def terms_body(order, own, factor, rows_in, factor_in, kept, far, near):
     width = kept.shape[0]
     for k, out in zip(order, (kept, near.at[:width], far, near.at[width:])):
         at = slice(k * width, (k + 1) * width)
-        total = dot(own[:, at], factor[...], 0, 0) + dot(rows[:, at], factor_in[...], 0, 0)
+        total = dot(own[:, at], factor[...], 0, 0) + dot(rows_in[:, at], factor_in[...], 0, 0)
         out[...] = total.astype(out.dtype)
 
 
-def pair_body(far, arrived, out):
-    out[...] = (far[...] + arrived[far.shape[0]:, :].astype(F32)).astype(BF)
+def pair_body(*refs):
+    *terms, out = refs
+    start = 0
+    for far, arrived in zip(terms[::2], terms[1::2]):
+        stop = start + far.shape[1]
+        out[:, start:stop] = (far[...] + arrived[far.shape[0]:, :].astype(F32)).astype(BF)
+        start = stop
 
 
 def total_of(kept, near, distant):
     return kept[...] + near[:kept.shape[0], :].astype(F32) + distant[...].astype(F32)
 
 
-def early_body(places, *refs):
-    first, second, (out, held, sems) = refs[:3], refs[3:6], refs[6:]
-    width = held.shape[2]
-    copies = []
-    for k, terms in enumerate((first, second)):
-        held[k] = total_of(*terms)
-        target = out.at[:, pl.ds(places[k] * width, width)]
-        copies.append(pltpu.make_async_copy(held.at[k], target, sems.at[k]))
-        copies[k].start()
-    for copy in copies:
-        copy.wait()
-
-
-def last_body(place, kept, near, distant, out_in, out, held, sem):
+def early_body(kept_a, near_a, kept_b, near_b, distant, *refs):
+    (*ups, out, held, sem) = refs
+    cut, hidden = kept_a.shape[1], distant.shape[1]
+    held[:, :cut] = total_of(kept_a, near_a, distant.at[:, :cut])
+    held[:, cut:hidden] = total_of(kept_b, near_b, distant.at[:, cut:])
+    held[:, hidden:] = total_of(*ups)
+    copy = pltpu.make_async_copy(held, out.at[:, pl.ds(0, held.shape[1])], sem)
+    copy.start()
+    copy.wait()
+
+
+def last_body(kept, near, distant, out_in, out, held, sem):
     held[...] = total_of(kept, near, distant)
     width = held.shape[1]
-    copy = pltpu.make_async_copy(held, out.at[:, pl.ds(place * width, width)], sem)
+    copy = pltpu.make_async_copy(held, out.at[:, pl.ds(out.shape[1] - width, width)], sem)
     copy.start()
     copy.wait()
 
@@ -263,58 +257,61 @@
     grad_blocks = exchange(sent[:experts], "expert", experts)
     scratch = [pltpu.VMEM((rows, width), BF)]
     side = shape((rows, half), BF)
-    early = experts // 2
-    part = shape((early * slots, half), BF)
     piece = share if staged else 0
     pre, act, own_rows, sent_rows = call(
         functools.partial(forward_body, experts, piece),
-        [shape((rows, 2 * hidden), F32), shape((rows, hidden), BF), side, part],
+        [shape((rows, 2 * hidden), F32), shape((rows, hidden), BF), side, side],
         (*token_blocks, gate_up), scratch, flops=4 * rows * hidden * width)
-    own_grads, late_grads, d_gate, d_up = call(
+    own_grads, sent_grads, d_first, d_gate, d_up = call(
         functools.partial(backward_body, experts, piece),
-        [side, side] + [shape((rows, hidden), BF)] * 2,
+        [side, side] + [shape((rows, k), BF) for k in (FIRST, hidden - FIRST, hidden)],
         (*grad_blocks, pre, down), scratch, flops=2 * rows * hidden * width)
     back = call(
         functools.partial(return_body, experts), [shape((2 * slots, width), BF)] * experts,
-        (act, d_gate, d_up, gate_up, down), flops=6 * rows * hidden * width)
+        (act, d_first, d_gate, d_up, gate_up, down), flops=6 * rows * hidden * width)
     if staged:
-        act_in = permute(act, "dp", shards, DOWN_PARTNER)
-        packed, = call(
-            functools.partial(pack_body, early, share), [part], token_blocks[:early],
-            [pltpu.VMEM((early * slots, width), BF)])
-        rows_in = [permute(packed, "dp", shards, UP_PARTNER), permute(sent_rows, "dp", shards, UP_PARTNER)]
-        grads_in = [permute(late_grads, "dp", shards, DOWN_PARTNER)]
+        rows_in = permute(sent_rows, "dp", shards, UP_PARTNER)
         d_gate_in = permute(d_gate, "dp", shards, UP_PARTNER)
         d_up_in = permute(d_up, "dp", shards, UP_PARTNER)
-        one = shape((share, hidden), F32)
-
-        def summed(own, factor, rows_in, factor_in, masks, order):
+        act_in = permute(act, "dp", shards, DOWN_PARTNER)
+        grads_in = permute(sent_grads, "dp", shards, DOWN_PARTNER)
+
+        def outs(columns):
+            return [shape((share, columns), F32)] * 2 + [shape((2 * share, columns), BF)]
+
+        def started(args, masks, order):
+            columns = args[1].shape[1]
             kept, far, near = call(
-                functools.partial(terms_body, order, len(rows_in)),
-                [one, one, shape((2 * share, hidden), BF)], (own, factor, *rows_in, factor_in),
-                [pltpu.VMEM((rows, half), BF)], flops=4 * rows * hidden * half)
-            near = permute(near, "dp", shards, masks[order[1]])
-            distant, = call(pair_body, [shape((share, hidden), BF)], (far, near))
-            return kept, near, permute(distant, "dp", shards, masks[order[2]])
-
-        gates = summed(own_rows, d_gate, rows_in, d_gate_in, UP_MASKS, GATE_ORDER)
-        downs = summed(own_grads, act, grads_in, act_in, DOWN_MASKS, DOWN_ORDER)
-        ups = summed(own_rows, d_up, rows_in, d_up_in, UP_MASKS, UP_ORDER)
+                functools.partial(terms_body, order), outs(columns), args,
+                flops=4 * rows * columns * half)
+            return kept, far, permute(near, "dp", shards, masks[order[1]])
+
+        def paired(terms, masks, order):
+            columns = sum(far.shape[1] for far in terms[::2])
+            distant, = call(pair_body, [shape((share, columns), BF)], terms)
+            return permute(distant, "dp", shards, masks[order[2]])
+
+        d_first_in = permute(d_first, "dp", shards, UP_PARTNER)
+        kept_a, far_a, near_a = started((own_rows, d_first, rows_in, d_first_in), UP_MASKS, GATE_ORDER)
+        kept_b, far_b, near_b = started((own_rows, d_gate, rows_in, d_gate_in), UP_MASKS, GATE_ORDER)
+        distant = paired((far_a, near_a, far_b, near_b), UP_MASKS, GATE_ORDER)
+        gates = (kept_a, near_a, kept_b, near_b, distant)
+        kept, far, near = started((own_rows, d_up, rows_in, d_up_in), UP_MASKS, UP_ORDER)
+        ups = (kept, near, paired((far, near), UP_MASKS, UP_ORDER))
+        kept, far, near = started((own_grads, act, grads_in, act_in), DOWN_MASKS, DOWN_ORDER)
+        downs = (kept, near, paired((far, near), DOWN_MASKS, DOWN_ORDER))
         whole = shape((share, 3 * hidden), F32)
-        terms = [gates, ups, downs]
-        first, second, final = FINISH
         weight_grad, = call(
-            functools.partial(early_body, (first, second)), [whole],
-            (*terms[first], *terms[second]),
-            [pltpu.VMEM((2, share, hidden), F32), pltpu.SemaphoreType.DMA((2,))], far_outs=(0,))
+            early_body, [whole], (*gates, *ups),
+            [pltpu.VMEM((share, 2 * hidden), F32), pltpu.SemaphoreType.DMA], far_outs=(0,))
         weight_grad, = call(
-            functools.partial(last_body, final), [whole], (*terms[final], weight_grad),
+            last_body, [whole], (*downs, weight_grad),
             [pltpu.VMEM((share, hidden), F32), pltpu.SemaphoreType.DMA],
             far_ins=(3,), far_outs=(0,), aliases={3: 0})
     else:
         weight_grad = lax.psum_scatter(
             jnp.concatenate([
-                dot(jnp.concatenate(token_blocks, axis=0), jnp.concatenate([d_gate, d_up], axis=1), 0, 0),
+                dot(jnp.concatenate(token_blocks, axis=0), jnp.concatenate([d_first, d_gate, d_up], axis=1), 0, 0),
                 dot(jnp.concatenate(grad_blocks, axis=0), act, 0, 0)], axis=1),
             "dp", scatter_dimension=0, tiled=True)
     returned = exchange(back, "expert", experts)
@@ -331,9 +328,10 @@
 
 DOWN_PARTNER, DOWN_MASKS = 1, (0, 2, 4, 6)
 UP_PARTNER, UP_MASKS = 2, (0, 1, 4, 5)
-FINISH = (0, 1, 2)
+FIRST = 128
 GATE_ORDER = (0, 2, 1, 3)
-DOWN_ORDER = UP_ORDER = (0, 1, 2, 3)
+DOWN_ORDER = (0, 1, 2, 3)
+UP_ORDER = (0, 1, 2, 3)
 
 
 def solution(mesh):

time: 50.5 us -> 56.8 us (1.12)
  waiting for transfers between devices: 15.8 us -> 25.4 us
  starting transfers between devices: 24.6 us -> 21.1 us
    ppermute x21 -> x22, waiting for transfers between devices: 15.8 us -> 25.4 us  [permute(): return lax.ppermute(array, axis, [(i, i ^ step) for i in range(size)])]
    ppermute x21 -> x22, starting transfers between devices: 24.6 us -> 21.1 us  [permute(): return lax.ppermute(array, axis, [(i, i ^ step) for i in range(size)])]
  transfers between devices with their start and end apart: 21 -> 22, of which waited for: 9 -> 10; matrix products, arithmetic and copies ran while one was open for 0% -> 0% of each run, Pallas kernels for 14% -> 12%
where the time goes in v2:
time: 56.8 us; the launch traced here: 56.6 us
  waiting for transfers between devices  25.4 us (45%)
  starting transfers between devices  21.1 us (37%)
  Pallas kernels  9.28 us (16%)
  between operations  0.81 us (1%)
    ppermute x22, waiting for transfers between devices, permute(): return lax.ppermute(array, axis, [(i, i ^ step) for i in range(size)])  25.4 us
    ppermute x22, starting transfers between devices, permute(): return lax.ppermute(array, axis, [(i, i ^ step) for i in range(size)])  21.1 us
    pallas_call x15, Pallas kernels, call(): pl.pallas_call(body, out_shape=list(outs), in_specs=[FAR if k in far_ins...  9.28 us
  transfers between devices with their start and end apart: 22, of which 10 were waited for; matrix products, arithmetic and copies ran while one was open for 0% of the time, Pallas kernels for 12%

profile of v2, /device:TPU:0, one launch (start us, length us, event | category | flops | bytes accessed | tf_op | source)
XLA Modules:
  0.0 56.6 jit_solution(13626820411674804104)
XLA Ops:
  0.6 1.2 %shard_map.93 = (bf16[192,128]{1,0:T(8,128)(2,1)S(1)}, bf16[48,1024]{1,0:T(8,128)(2,1)S(1)}, bf16[48,1024]{1,0:T(8,128)(2,1)S(1)}, bf16[48,1024]{1,0:T(8,128)(2,1)S(1)}, bf16[48,1024]{1,0:T(8,128)(2,1)S(1)}) custom-call(s32[1,128]{1,0:T(1,128)} %bitcast.7, bf16[128,1024]{1,0:T(8,128)(2,1)} %tokens_in.1), custom_call_target="tpu_custom_call" | custom-call | flops 50331648 | bytes 705024 | tf_op jit(solution)/shard_map/pallas_call | solution.py:27
  1.9 0.6 collective-permute-start
  2.4 2.6 %collective-permute-start.1 = (bf16[48,1024]{1,0:T(8,128)(2,1)S(1)}, bf16[48,1024]{1,0:T(8,128)(2,1)S(1)}, u32[]{:S(2)}, u32[]{:S(2)}) collective-permute-start(bf16[48,1024]{1,0:T(8,128)(2,1)S(1)} %get-tuple-element.45), channel_id=1, source_target_pairs={{0,2},{1,3},{2,0},{3,1},{4,6},{5,7},{6,4},{7,5},{8,10},{9,11},{10,... | collective-permute-start | bytes 294920 | tf_op jit(solution)/shard_map/ppermute | solution.py:222
  5.0 0.0 collective-permute-start.2
  5.0 1.7 %shard_map.94 = (bf16[1,1024,768]{2,1,0:T(8,128)(2,1)S(1)}, bf16[1,384,1024]{2,1,0:T(8,128)(2,1)S(1)}, bf16[48,1024]{1,0:T(8,128)(2,1)S(1)}, bf16[48,1024]{1,0:T...) custom-call(bf16[192,128]{1,0:T(8,128)(2,1)S(1)} %get-tuple-element.47.refs_0_.refs_4_, ...), custom_call_target="tpu_custom_call" | custom-call | flops 50331648 | bytes 5423616 | tf_op jit(solution)/shard_map/pallas_call | solution.py:27
  6.8 0.2 collective-permute-start.3
  7.0 1.9 %collective-permute-start.4 = (bf16[48,1024]{1,0:T(8,128)(2,1)S(1)}, bf16[48,1024]{1,0:T(8,128)(2,1)S(1)}, u32[]{:S(2)}, u32[]{:S(2)}) collective-permute-start(bf16[48,1024]{1,0:T(8,128)(2,1)S(1)} %get-tuple-element.52), channel_id=1, source_target_pairs={{0,2},{1,3},{2,0},{3,1},{4,6},{5,7},{6,4},{7,5},{8,10},{9,11},{10,... | collective-permute-start | bytes 294920 | tf_op jit(solution)/shard_map/ppermute | solution.py:222
  8.9 0.0 collective-permute-done.refs_1_
  8.9 0.0 collective-permute-start.5
  9.0 0.0 collective-permute-done.1.refs_2_
  9.0 1.3 %collective-permute-done.2.refs_3_ = bf16[48,1024]{1,0:T(8,128)(2,1)S(1)} collective-permute-done((bf16[48,1024]{1,0:T(8,128)(2,1)S(1)}, bf16[48,1024]{1,0:T(8,128)(2,1)S(1)}, u32[]{:S(2)}, u32[]{:S(2)}) %collective-permute-start.2) | collective-permute-done | bytes 98336 | tf_op jit(solution)/shard_map/ppermute | solution.py:222
  10.3 0.6 shard_map.95
  10.9 2.0 %collective-permute-done.4.refs_2_ = bf16[48,1024]{1,0:T(8,128)(2,1)S(1)} collective-permute-done((bf16[48,1024]{1,0:T(8,128)(2,1)S(1)}, bf16[48,1024]{1,0:T(8,128)(2,1)S(1)}, u32[]{:S(2)}, u32[]{:S(2)}) %collective-permute-start.4) | collective-permute-done | bytes 98336 | tf_op jit(solution)/shard_map/ppermute | solution.py:222
  12.9 1.6 %collective-permute-done.5.refs_3_ = bf16[48,1024]{1,0:T(8,128)(2,1)S(1)} collective-permute-done((bf16[48,1024]{1,0:T(8,128)(2,1)S(1)}, bf16[48,1024]{1,0:T(8,128)(2,1)S(1)}, u32[]{:S(2)}, u32[]{:S(2)}) %collective-permute-start.5) | collective-permute-done | bytes 98336 | tf_op jit(solution)/shard_map/ppermute | solution.py:222
  14.4 0.5 shard_map.96
  15.0 1.6 %collective-permute-start.9 = (bf16[192,512]{1,0:T(8,128)(2,1)S(1)}, bf16[192,512]{1,0:T(8,128)(2,1)S(1)}, u32[]{:S(2)}, u32[]{:S(2)}) collective-permute-start(bf16[192,512]{1,0:T(8,128)(2,1)S(1)} %get-tuple-element.67), channel_id=1, source_target_pairs={{0,4},{4,0},{8,12},{12,8},{16,20},{20,16},{24,28},{28,24},{1,5},{5... | collective-permute-start | bytes 589832 | tf_op jit(solution)/shard_map/ppermute | solution.py:222
  16.5 1.6 %collective-permute-start.13 = (bf16[192,512]{1,0:T(8,128)(2,1)S(1)}, bf16[192,512]{1,0:T(8,128)(2,1)S(1)}, u32[]{:S(2)}, u32[]{:S(2)}) collective-permute-start(bf16[192,512]{1,0:T(8,128)(2,1)S(1)} %get-tuple-element.72), channel_id=1, source_target_pairs={{0,8},{4,12},{8,0},{12,4},{16,24},{20,28},{24,16},{28,20},{1,9},{5... | collective-permute-start | bytes 589832 | tf_op jit(solution)/shard_map/ppermute | solution.py:222
  18.1 0.5 collective-permute-start.10
  18.6 0.5 collective-permute-start.19
  19.1 1.6 %collective-permute-start.16 = (bf16[192,256]{1,0:T(8,128)(2,1)S(1)}, bf16[192,256]{1,0:T(8,128)(2,1)S(1)}, u32[]{:S(2)}, u32[]{:S(2)}) collective-permute-start(bf16[192,256]{1,0:T(8,128)(2,1)S(1)} %get-tuple-element.57.d_gate.factor), channel_id=1, source_target_pairs={{0,8},{4,12},{8,0},{12,4},{16,24},{20,28},{24,16},{28,20},{1,9},{5... | collective-permute-start | bytes 294920 | tf_op jit(solution)/shard_map/ppermute | solution.py:222
  20.6 4.5 %collective-permute-done.10.factor_in = bf16[192,384]{1,0:T(8,128)(2,1)S(1)} collective-permute-done((bf16[192,384]{1,0:T(8,128)(2,1)S(1)}, bf16[192,384]{1,0:T(8,128)(2,1)S(1)}, u32[]{:S(2)}, u32[]{:S(2)}) %collective-permute-start.10) | collective-permute-done | bytes 147488 | tf_op jit(solution)/shard_map/ppermute | solution.py:222
  25.1 1.8 %collective-permute-start.14 = (bf16[192,128]{1,0:T(8,128)(2,1)S(1)}, bf16[192,128]{1,0:T(8,128)(2,1)S(1)}, u32[]{:S(2)}, u32[]{:S(2)}) collective-permute-start(bf16[192,128]{1,0:T(8,128)(2,1)S(1)} %get-tuple-element.56.d_first.factor), channel_id=1, source_target_pairs={{0,8},{4,12},{8,0},{12,4},{16,24},{20,28},{24,16},{28,20},{1,9},{5... | collective-permute-start | bytes 147464 | tf_op jit(solution)/shard_map/ppermute | solution.py:222
  26.9 0.0 collective-permute-done.9.rows_in
  26.9 0.5 shard_map.99
  27.4 0.3 collective-permute-start.11
  27.7 1.5 %collective-permute-done.16.factor_in = bf16[192,256]{1,0:T(8,128)(2,1)S(1)} collective-permute-done((bf16[192,256]{1,0:T(8,128)(2,1)S(1)}, bf16[192,256]{1,0:T(8,128)(2,1)S(1)}, u32[]{:S(2)}, u32[]{:S(2)}) %collective-permute-start.16) | collective-permute-done | bytes 98336 | tf_op jit(solution)/shard_map/ppermute | solution.py:222
  29.2 0.3 shard_map.102
  29.5 2.7 %collective-permute-start.17 = (bf16[256,256]{1,0:T(8,128)(2,1)S(1)}, bf16[256,256]{1,0:T(8,128)(2,1)S(1)}, u32[]{:S(2)}, u32[]{:S(2)}) collective-permute-start(bf16[256,256]{1,0:T(8,128)(2,1)S(1)} %get-tuple-element.76), channel_id=1, source_target_pairs={{0,16},{4,20},{8,24},{12,28},{16,0},{20,4},{24,8},{28,12},{1,17},{... | collective-permute-start | bytes 393224 | tf_op jit(solution)/shard_map/ppermute | solution.py:222
  32.2 0.5 shard_map.104
  32.7 0.3 collective-permute-start.20
  33.0 0.9 %shard_map.97 = (bf16[96,1024]{1,0:T(8,128)(2,1)S(1)}, bf16[96,1024]{1,0:T(8,128)(2,1)S(1)}, bf16[96,1024]{1,0:T(8,128)(2,1)S(1)}, bf16[96,1024]{1,0:T(8,128)(2,1)S(1)}) custom-call(bf16[192,384]{1,0:T(8,128)(2,1)S(1)} %get-tuple-element.49.act.factor, bf16[192,128]{1,0:T(8,128)(2,1)S(1)} %get-tuple-element.56.d_first.factor, ...), custom_call_target="tpu_custom_call" | custom-call | flops 452984832 | bytes 3588096 | tf_op jit(solution)/shard_map/pallas_call | solution.py:27
  33.9 0.0 copy-start
  33.9 0.0 copy-start.1
  33.9 0.1 collective-permute-start.6
  34.0 0.3 shard_map.101
  34.3 0.4 collective-permute-start.15
  34.7 6.8 %collective-permute-done.15.refs_1_.near_a = bf16[256,128]{1,0:T(8,128)(2,1)S(1)} collective-permute-done((bf16[256,128]{1,0:T(8,128)(2,1)S(1)}, bf16[256,128]{1,0:T(8,128)(2,1)S(1)}, u32[]{:S(2)}, u32[]{:S(2)}) %collective-permute-start.15) | collective-permute-done | bytes 65568 | tf_op jit(solution)/shard_map/ppermute | solution.py:222
  41.6 1.5 %collective-permute-start.7 = (bf16[96,1024]{1,0:T(8,128)(2,1)S(1)}, bf16[96,1024]{1,0:T(8,128)(2,1)S(1)}, u32[]{:S(2)}, u32[]{:S(2)}) collective-permute-start(bf16[96,1024]{1,0:T(8,128)(2,1)S(1)} %get-tuple-element.61), channel_id=1, source_target_pairs={{0,2},{1,3},{2,0},{3,1},{4,6},{5,7},{6,4},{7,5},{8,10},{9,11},{10,... | collective-permute-start | bytes 589832 | tf_op jit(solution)/shard_map/ppermute | solution.py:222
  43.1 0.1 collective-permute-start.18
  43.2 0.5 collective-permute-start.21
  43.8 2.6 %collective-permute-start.12 = (bf16[128,384]{1,0:T(8,128)(2,1)S(1)}, bf16[128,384]{1,0:T(8,128)(2,1)S(1)}, u32[]{:S(2)}, u32[]{:S(2)}) collective-permute-start(bf16[128,384]{1,0:T(8,128)(2,1)S(1)} %shard_map.100), channel_id=1, source_target_pairs={{0,16},{4,20},{8,24},{12,28},{16,0},{20,4},{24,8},{28,12},{1,17},{... | collective-permute-start | bytes 294920 | tf_op jit(solution)/shard_map/ppermute | solution.py:222
  46.3 3.0 %collective-permute-done.7.refs_2_ = bf16[96,1024]{1,0:T(8,128)(2,1)S(1)} collective-permute-done((bf16[96,1024]{1,0:T(8,128)(2,1)S(1)}, bf16[96,1024]{1,0:T(8,128)(2,1)S(1)}, u32[]{:S(2)}, u32[]{:S(2)}) %collective-permute-start.7) | collective-permute-done | bytes 196640 | tf_op jit(solution)/shard_map/ppermute | solution.py:222
  49.4 2.3 %collective-permute-done.8.refs_3_ = bf16[96,1024]{1,0:T(8,128)(2,1)S(1)} collective-permute-done((bf16[96,1024]{1,0:T(8,128)(2,1)S(1)}, bf16[96,1024]{1,0:T(8,128)(2,1)S(1)}, u32[]{:S(2)}, u32[]{:S(2)}) %collective-permute-start.8) | collective-permute-done | bytes 196640 | tf_op jit(solution)/shard_map/ppermute | solution.py:222
  51.7 1.1 %shard_map.98 = (bf16[128,1024]{1,0:T(8,128)(2,1)}, bf16[128,1024]{1,0:T(8,128)(2,1)}, f32[1,128]{1,0:T(1,128)}) custom-call(bf16[96,1024]{1,0:T(8,128)(2,1)S(1)} %get-tuple-element.59.refs_0_, bf16[96,1024]{1,0:T(8,128)(2,1)S(1)} %collective-permute-done.6.refs_1_, bf16[96,1024]{1,0:T(8,128)(2,1)S(1)} %collective-permute-done.7.refs_2_, ...), custom_call_target="tpu_custom_call" | custom-call | flops 100663296 | bytes 1623040 | tf_op jit(solution)/shard_map/pallas_call | solution.py:27
  52.8 1.3 %collective-permute-done.21.refs_2_ = bf16[128,384]{1,0:T(8,128)(2,1)S(1)} collective-permute-done((bf16[128,384]{1,0:T(8,128)(2,1)S(1)}, bf16[128,384]{1,0:T(8,128)(2,1)S(1)}, u32[]{:S(2)}, u32[]{:S(2)}) %collective-permute-start.21) | collective-permute-done | bytes 98336 | tf_op jit(solution)/shard_map/ppermute | solution.py:222
  54.1 0.8 %shard_map.106.out_in = f32[128,1152]{1,0:T(8,128)} custom-call(f32[128,128]{1,0:T(8,128)S(1)} %get-tuple-element.73.kept_a, bf16[256,128]{1,0:T(8,128)(2,1)S(1)} %collective-permute-done.15.refs_1_.near_a, f32[128,256]{1,0:T(8,128)S(1)} %get-tuple-element.75.kept_b, bf16[256,256]{1,0:T(8,128)(2,1)S(1)} %collective-permute-done.17.refs_3_.near_b, ...), custom_call_target="tpu_custom_call" | custom-call | bytes 1572864 | tf_op jit(solution)/shard_map/pallas_call | solution.py:27
  54.9 1.0 %collective-permute-done.12.distant = bf16[128,384]{1,0:T(8,128)(2,1)S(1)} collective-permute-done((bf16[128,384]{1,0:T(8,128)(2,1)S(1)}, bf16[128,384]{1,0:T(8,128)(2,1)S(1)}, u32[]{:S(2)}, u32[]{:S(2)}) %collective-permute-start.12) | collective-permute-done | bytes 98336 | tf_op jit(solution)/shard_map/ppermute | solution.py:222
  55.9 0.7 %shard_map.107 = f32[128,1152]{1,0:T(8,128)} custom-call(f32[128,384]{1,0:T(8,128)S(1)} %get-tuple-element.68.kept, bf16[256,384]{1,0:T(8,128)(2,1)S(1)} %collective-permute-done.11.refs_1_.near, bf16[128,384]{1,0:T(8,128)(2,1)S(1)} %collective-permute-done.12.distant, f32[128,1152]{1,0:T(8,128)} %shard_map.106.out_in), custom_call_target="tpu_custom_call", output_to_operand_aliasing={{}: (3, {})} | custom-call | bytes 1671168 | tf_op jit(solution)/shard_map/pallas_call | solution.py:27
  (15 shorter events, 0.1 us)
Async XLA Ops:
  1.9 7.1 %collective-permute-start = (bf16[48,1024]{1,0:T(8,128)(2,1)S(1)}, bf16[48,1024]{1,0:T(8,128)(2,1)S(1)}, u32[]{:S(2)}, u32[]{:S(2)}) collective-permute-start(bf16[48,1024]{1,0:T(8,128)(2,1)S(1)} %get-tuple-element.44), channel_id=1, source_target_pairs={{0,1},{1,0},{2,3},{3,2},{4,5},{5,4},{6,7},{7,6},{8,9},{9,8},{10,11... | collective-permute-start | bytes 294920 | tf_op jit(solution)/shard_map/ppermute | solution.py:222
  2.4 6.5 %collective-permute-start.1 = (bf16[48,1024]{1,0:T(8,128)(2,1)S(1)}, bf16[48,1024]{1,0:T(8,128)(2,1)S(1)}, u32[]{:S(2)}, u32[]{:S(2)}) collective-permute-start(bf16[48,1024]{1,0:T(8,128)(2,1)S(1)} %get-tuple-element.45), channel_id=1, source_target_pairs={{0,2},{1,3},{2,0},{3,1},{4,6},{5,7},{6,4},{7,5},{8,10},{9,11},{10,... | collective-permute-start | bytes 294920 | tf_op jit(solution)/shard_map/ppermute | solution.py:222
  5.0 5.3 %collective-permute-start.2 = (bf16[48,1024]{1,0:T(8,128)(2,1)S(1)}, bf16[48,1024]{1,0:T(8,128)(2,1)S(1)}, u32[]{:S(2)}, u32[]{:S(2)}) collective-permute-start(bf16[48,1024]{1,0:T(8,128)(2,1)S(1)} %get-tuple-element.46), channel_id=1, source_target_pairs={{0,3},{1,2},{2,1},{3,0},{4,7},{5,6},{6,5},{7,4},{8,11},{9,10},{10,... | collective-permute-start | bytes 294920 | tf_op jit(solution)/shard_map/ppermute | solution.py:222
  6.8 4.1 %collective-permute-start.3 = (bf16[48,1024]{1,0:T(8,128)(2,1)S(1)}, bf16[48,1024]{1,0:T(8,128)(2,1)S(1)}, u32[]{:S(2)}, u32[]{:S(2)}) collective-permute-start(bf16[48,1024]{1,0:T(8,128)(2,1)S(1)} %get-tuple-element.51), channel_id=1, source_target_pairs={{0,1},{1,0},{2,3},{3,2},{4,5},{5,4},{6,7},{7,6},{8,9},{9,8},{10,11... | collective-permute-start | bytes 294920 | tf_op jit(solution)/shard_map/ppermute | solution.py:222
  7.0 5.9 %collective-permute-start.4 = (bf16[48,1024]{1,0:T(8,128)(2,1)S(1)}, bf16[48,1024]{1,0:T(8,128)(2,1)S(1)}, u32[]{:S(2)}, u32[]{:S(2)}) collective-permute-start(bf16[48,1024]{1,0:T(8,128)(2,1)S(1)} %get-tuple-element.52), channel_id=1, source_target_pairs={{0,2},{1,3},{2,0},{3,1},{4,6},{5,7},{6,4},{7,5},{8,10},{9,11},{10,... | collective-permute-start | bytes 294920 | tf_op jit(solution)/shard_map/ppermute | solution.py:222
  8.9 5.5 %collective-permute-start.5 = (bf16[48,1024]{1,0:T(8,128)(2,1)S(1)}, bf16[48,1024]{1,0:T(8,128)(2,1)S(1)}, u32[]{:S(2)}, u32[]{:S(2)}) collective-permute-start(bf16[48,1024]{1,0:T(8,128)(2,1)S(1)} %get-tuple-element.53), channel_id=1, source_target_pairs={{0,3},{1,2},{2,1},{3,0},{4,7},{5,6},{6,5},{7,4},{8,11},{9,10},{10,... | collective-permute-start | bytes 294920 | tf_op jit(solution)/shard_map/ppermute | solution.py:222
  15.0 12.0 %collective-permute-start.9 = (bf16[192,512]{1,0:T(8,128)(2,1)S(1)}, bf16[192,512]{1,0:T(8,128)(2,1)S(1)}, u32[]{:S(2)}, u32[]{:S(2)}) collective-permute-start(bf16[192,512]{1,0:T(8,128)(2,1)S(1)} %get-tuple-element.67), channel_id=1, source_target_pairs={{0,4},{4,0},{8,12},{12,8},{16,20},{20,16},{24,28},{28,24},{1,5},{5... | collective-permute-start | bytes 589832 | tf_op jit(solution)/shard_map/ppermute | solution.py:222
  16.5 12.7 %collective-permute-start.13 = (bf16[192,512]{1,0:T(8,128)(2,1)S(1)}, bf16[192,512]{1,0:T(8,128)(2,1)S(1)}, u32[]{:S(2)}, u32[]{:S(2)}) collective-permute-start(bf16[192,512]{1,0:T(8,128)(2,1)S(1)} %get-tuple-element.72), channel_id=1, source_target_pairs={{0,8},{4,12},{8,0},{12,4},{16,24},{20,28},{24,16},{28,20},{1,9},{5... | collective-permute-start | bytes 589832 | tf_op jit(solution)/shard_map/ppermute | solution.py:222
  18.1 7.0 %collective-permute-start.10 = (bf16[192,384]{1,0:T(8,128)(2,1)S(1)}, bf16[192,384]{1,0:T(8,128)(2,1)S(1)}, u32[]{:S(2)}, u32[]{:S(2)}) collective-permute-start(bf16[192,384]{1,0:T(8,128)(2,1)S(1)} %get-tuple-element.49.act.factor), channel_id=1, source_target_pairs={{0,4},{4,0},{8,12},{12,8},{16,20},{20,16},{24,28},{28,24},{1,5},{5... | collective-permute-start | bytes 442376 | tf_op jit(solution)/shard_map/ppermute | solution.py:222
  18.6 13.6 %collective-permute-start.19 = (bf16[192,384]{1,0:T(8,128)(2,1)S(1)}, bf16[192,384]{1,0:T(8,128)(2,1)S(1)}, u32[]{:S(2)}, u32[]{:S(2)}) collective-permute-start(bf16[192,384]{1,0:T(8,128)(2,1)S(1)} %get-tuple-element.58.d_up.factor), channel_id=1, source_target_pairs={{0,8},{4,12},{8,0},{12,4},{16,24},{20,28},{24,16},{28,20},{1,9},{5... | collective-permute-start | bytes 442376 | tf_op jit(solution)/shard_map/ppermute | solution.py:222
  19.1 10.1 %collective-permute-start.16 = (bf16[192,256]{1,0:T(8,128)(2,1)S(1)}, bf16[192,256]{1,0:T(8,128)(2,1)S(1)}, u32[]{:S(2)}, u32[]{:S(2)}) collective-permute-start(bf16[192,256]{1,0:T(8,128)(2,1)S(1)} %get-tuple-element.57.d_gate.factor), channel_id=1, source_target_pairs={{0,8},{4,12},{8,0},{12,4},{16,24},{20,28},{24,16},{28,20},{1,9},{5... | collective-permute-start | bytes 294920 | tf_op jit(solution)/shard_map/ppermute | solution.py:222
  25.1 8.9 %collective-permute-start.14 = (bf16[192,128]{1,0:T(8,128)(2,1)S(1)}, bf16[192,128]{1,0:T(8,128)(2,1)S(1)}, u32[]{:S(2)}, u32[]{:S(2)}) collective-permute-start(bf16[192,128]{1,0:T(8,128)(2,1)S(1)} %get-tuple-element.56.d_first.factor), channel_id=1, source_target_pairs={{0,8},{4,12},{8,0},{12,4},{16,24},{20,28},{24,16},{28,20},{1,9},{5... | collective-permute-start | bytes 147464 | tf_op jit(solution)/shard_map/ppermute | solution.py:222
  27.4 15.8 %collective-permute-start.11 = (bf16[256,384]{1,0:T(8,128)(2,1)S(1)}, bf16[256,384]{1,0:T(8,128)(2,1)S(1)}, u32[]{:S(2)}, u32[]{:S(2)}) collective-permute-start(bf16[256,384]{1,0:T(8,128)(2,1)S(1)} %get-tuple-element.69), channel_id=1, source_target_pairs={{0,8},{4,12},{8,0},{12,4},{16,24},{20,28},{24,16},{28,20},{1,9},{5... | collective-permute-start | bytes 589832 | tf_op jit(solution)/shard_map/ppermute | solution.py:222
  29.5 13.5 %collective-permute-start.17 = (bf16[256,256]{1,0:T(8,128)(2,1)S(1)}, bf16[256,256]{1,0:T(8,128)(2,1)S(1)}, u32[]{:S(2)}, u32[]{:S(2)}) collective-permute-start(bf16[256,256]{1,0:T(8,128)(2,1)S(1)} %get-tuple-element.76), channel_id=1, source_target_pairs={{0,16},{4,20},{8,24},{12,28},{16,0},{20,4},{24,8},{28,12},{1,17},{... | collective-permute-start | bytes 393224 | tf_op jit(solution)/shard_map/ppermute | solution.py:222
  32.7 10.4 %collective-permute-start.20 = (bf16[256,384]{1,0:T(8,128)(2,1)S(1)}, bf16[256,384]{1,0:T(8,128)(2,1)S(1)}, u32[]{:S(2)}, u32[]{:S(2)}) collective-permute-start(bf16[256,384]{1,0:T(8,128)(2,1)S(1)} %get-tuple-element.80), channel_id=1, source_target_pairs={{0,4},{4,0},{8,12},{12,8},{16,20},{20,16},{24,28},{28,24},{1,5},{5... | collective-permute-start | bytes 589832 | tf_op jit(solution)/shard_map/ppermute | solution.py:222
  33.9 17.8 %copy-start = (bf16[128,1024]{1,0:T(8,128)(2,1)S(1)}, bf16[128,1024]{1,0:T(8,128)(2,1)}, u32[]{:S(2)}) copy-start(bf16[128,1024]{1,0:T(8,128)(2,1)} %refs_6_.1) | copy-start | bytes 786436
  33.9 17.8 %copy-start.1 = (f32[128,1]{0,1:T(1,128)S(1)}, f32[128,1]{0,1:T(1,128)}, u32[]{:S(2)}) copy-start(f32[128,1]{0,1:T(1,128)} %param.8) | copy-start | bytes 1540
  33.9 9.8 %collective-permute-start.6 = (bf16[96,1024]{1,0:T(8,128)(2,1)S(1)}, bf16[96,1024]{1,0:T(8,128)(2,1)S(1)}, u32[]{:S(2)}, u32[]{:S(2)}) collective-permute-start(bf16[96,1024]{1,0:T(8,128)(2,1)S(1)} %get-tuple-element.60), channel_id=1, source_target_pairs={{0,1},{1,0},{2,3},{3,2},{4,5},{5,4},{6,7},{7,6},{8,9},{9,8},{10,11... | collective-permute-start | bytes 589832 | tf_op jit(solution)/shard_map/ppermute | solution.py:222
  34.3 7.2 %collective-permute-start.15 = (bf16[256,128]{1,0:T(8,128)(2,1)S(1)}, bf16[256,128]{1,0:T(8,128)(2,1)S(1)}, u32[]{:S(2)}, u32[]{:S(2)}) collective-permute-start(bf16[256,128]{1,0:T(8,128)(2,1)S(1)} %get-tuple-element.74), channel_id=1, source_target_pairs={{0,16},{4,20},{8,24},{12,28},{16,0},{20,4},{24,8},{28,12},{1,17},{... | collective-permute-start | bytes 196616 | tf_op jit(solution)/shard_map/ppermute | solution.py:222
  41.6 7.8 %collective-permute-start.7 = (bf16[96,1024]{1,0:T(8,128)(2,1)S(1)}, bf16[96,1024]{1,0:T(8,128)(2,1)S(1)}, u32[]{:S(2)}, u32[]{:S(2)}) collective-permute-start(bf16[96,1024]{1,0:T(8,128)(2,1)S(1)} %get-tuple-element.61), channel_id=1, source_target_pairs={{0,2},{1,3},{2,0},{3,1},{4,6},{5,7},{6,4},{7,5},{8,10},{9,11},{10,... | collective-permute-start | bytes 589832 | tf_op jit(solution)/shard_map/ppermute | solution.py:222
  43.1 8.6 %collective-permute-start.8 = (bf16[96,1024]{1,0:T(8,128)(2,1)S(1)}, bf16[96,1024]{1,0:T(8,128)(2,1)S(1)}, u32[]{:S(2)}, u32[]{:S(2)}) collective-permute-start(bf16[96,1024]{1,0:T(8,128)(2,1)S(1)} %get-tuple-element.62), channel_id=1, source_target_pairs={{0,3},{1,2},{2,1},{3,0},{4,7},{5,6},{6,5},{7,4},{8,11},{9,10},{10,... | collective-permute-start | bytes 589832 | tf_op jit(solution)/shard_map/ppermute | solution.py:222
  43.1 9.7 %collective-permute-start.18 = (bf16[128,384]{1,0:T(8,128)(2,1)S(1)}, bf16[128,384]{1,0:T(8,128)(2,1)S(1)}, u32[]{:S(2)}, u32[]{:S(2)}) collective-permute-start(bf16[128,384]{1,0:T(8,128)(2,1)S(1)} %shard_map.103), channel_id=1, source_target_pairs={{0,4},{4,0},{8,12},{12,8},{16,20},{20,16},{24,28},{28,24},{1,5},{5... | collective-permute-start | bytes 294920 | tf_op jit(solution)/shard_map/ppermute | solution.py:222
  43.2 10.8 %collective-permute-start.21 = (bf16[128,384]{1,0:T(8,128)(2,1)S(1)}, bf16[128,384]{1,0:T(8,128)(2,1)S(1)}, u32[]{:S(2)}, u32[]{:S(2)}) collective-permute-start(bf16[128,384]{1,0:T(8,128)(2,1)S(1)} %shard_map.105), channel_id=1, source_target_pairs={{0,16},{4,20},{8,24},{12,28},{16,0},{20,4},{24,8},{28,12},{1,17},{... | collective-permute-start | bytes 294920 | tf_op jit(solution)/shard_map/ppermute | solution.py:222
  43.8 12.1 %collective-permute-start.12 = (bf16[128,384]{1,0:T(8,128)(2,1)S(1)}, bf16[128,384]{1,0:T(8,128)(2,1)S(1)}, u32[]{:S(2)}, u32[]{:S(2)}) collective-permute-start(bf16[128,384]{1,0:T(8,128)(2,1)S(1)} %shard_map.100), channel_id=1, source_target_pairs={{0,16},{4,20},{8,24},{12,28},{16,0},{20,4},{24,8},{28,12},{1,17},{... | collective-permute-start | bytes 294920 | tf_op jit(solution)/shard_map/ppermute | solution.py:222

commit v3 on v2

--- a/solution.py
+++ b/solution.py
@@ -54,16 +54,13 @@
     return jnp.sum(jnp.where(at == to, jnp.broadcast_to(column, (count, count)), 0.0), axis=0, keepdims=True)
 
 
-def one_hot(ids, experts, slots):
+def one_hot(ids, earlier, experts, slots):
     me = lax.axis_index("expert")
     count = ids.shape[1]
     padded = max(8, experts)
     kinds = lax.broadcasted_iota(jnp.int32, (padded, count), 0)
     here = kinds == jnp.broadcast_to(ids, (padded, count))
     onehot = jnp.where(here, 1.0, 0.0)
-    at = lax.broadcasted_iota(jnp.int32, (count, count), 0)
-    to = lax.broadcasted_iota(jnp.int32, (count, count), 1)
-    earlier = jnp.where(at < to, 1.0, 0.0).astype(BF)
     before = dot(onehot.astype(BF), earlier, 1, 0)
     position = jnp.sum(before * onehot, axis=0, keepdims=True).astype(jnp.int32)
     slot = (ids ^ me) * slots + position
@@ -82,8 +79,12 @@
 def tokens_body(experts, slots, ids_in, tokens_in, placed_out, *refs):
     blocks, (ids, tokens, sems) = refs[:experts], refs[experts:]
     copies = copy_in((ids_in, tokens_in), (ids, tokens), sems)
+    count = ids.shape[1]
+    at = lax.broadcasted_iota(jnp.int32, (count, count), 0)
+    to = lax.broadcasted_iota(jnp.int32, (count, count), 1)
+    earlier = jnp.where(at < to, 1.0, 0.0).astype(BF)
     copies[0].wait()
-    placed = one_hot(ids[...], experts, slots)
+    placed = one_hot(ids[...], earlier, experts, slots)
     placed_out[...] = placed
     copies[1].wait()
     sent = dot(placed, tokens[...], 1, 0).astype(BF)
@@ -195,12 +196,17 @@
     copy.wait()
 
 
-def last_body(kept, near, distant, out_in, out, held, sem):
-    held[...] = total_of(kept, near, distant)
-    width = held.shape[1]
-    copy = pltpu.make_async_copy(held, out.at[:, pl.ds(out.shape[1] - width, width)], sem)
-    copy.start()
-    copy.wait()
+def last_body(kept, near, distant, out_in, out, held, sems):
+    count, width = held.shape
+    copies = []
+    for k in range(2):
+        part = slice(k * count // 2, (k + 1) * count // 2)
+        held[part] = kept[part] + near[part].astype(F32) + distant[part].astype(F32)
+        target = out.at[part, pl.ds(out.shape[1] - width, width)]
+        copies.append(pltpu.make_async_copy(held.at[part], target, sems.at[k]))
+        copies[k].start()
+    for copy in copies:
+        copy.wait()
 
 
 def combine_body(experts, *refs):
@@ -306,7 +312,7 @@
             [pltpu.VMEM((share, 2 * hidden), F32), pltpu.SemaphoreType.DMA], far_outs=(0,))
         weight_grad, = call(
             last_body, [whole], (*downs, weight_grad),
-            [pltpu.VMEM((share, hidden), F32), pltpu.SemaphoreType.DMA],
+            [pltpu.VMEM((share, hidden), F32), pltpu.SemaphoreType.DMA((2,))],
             far_ins=(3,), far_outs=(0,), aliases={3: 0})
     else:
         weight_grad = lax.psum_scatter(

time: 56.8 us -> 56.7 us (level)
  no operation moved by 1% of the time
where the time goes in v3:
time: 56.7 us; the launch traced here: 56.6 us
  waiting for transfers between devices  25.4 us (45%)
  starting transfers between devices  21.1 us (37%)
  Pallas kernels  9.27 us (16%)
  between operations  0.81 us (1%)
    ppermute x22, waiting for transfers between devices, permute(): return lax.ppermute(array, axis, [(i, i ^ step) for i in range(size)])  25.4 us
    ppermute x22, starting transfers between devices, permute(): return lax.ppermute(array, axis, [(i, i ^ step) for i in range(size)])  21.1 us
    pallas_call x15, Pallas kernels, call(): pl.pallas_call(body, out_shape=list(outs), in_specs=[FAR if k in far_ins...  9.27 us
  transfers between devices with their start and end apart: 22, of which 10 were waited for; matrix products, arithmetic and copies ran while one was open for 0% of the time, Pallas kernels for 12%

profile of v3, /device:TPU:0, one launch (start us, length us, event | category | flops | bytes accessed | tf_op | source)
XLA Modules:
  0.0 56.6 jit_solution(14258193601837283839)
XLA Ops:
  0.6 1.2 %shard_map.93 = (bf16[192,128]{1,0:T(8,128)(2,1)S(1)}, bf16[48,1024]{1,0:T(8,128)(2,1)S(1)}, bf16[48,1024]{1,0:T(8,128)(2,1)S(1)}, bf16[48,1024]{1,0:T(8,128)(2,1)S(1)}, bf16[48,1024]{1,0:T(8,128)(2,1)S(1)}) custom-call(s32[1,128]{1,0:T(1,128)} %bitcast.7, bf16[128,1024]{1,0:T(8,128)(2,1)} %tokens_in.1), custom_call_target="tpu_custom_call" | custom-call | flops 50331648 | bytes 705024 | tf_op jit(solution)/shard_map/pallas_call | solution.py:27
  1.9 0.6 collective-permute-start
  2.4 2.6 %collective-permute-start.1 = (bf16[48,1024]{1,0:T(8,128)(2,1)S(1)}, bf16[48,1024]{1,0:T(8,128)(2,1)S(1)}, u32[]{:S(2)}, u32[]{:S(2)}) collective-permute-start(bf16[48,1024]{1,0:T(8,128)(2,1)S(1)} %get-tuple-element.45), channel_id=1, source_target_pairs={{0,2},{1,3},{2,0},{3,1},{4,6},{5,7},{6,4},{7,5},{8,10},{9,11},{10,... | collective-permute-start | bytes 294920 | tf_op jit(solution)/shard_map/ppermute | solution.py:228
  5.0 0.0 collective-permute-start.2
  5.0 1.7 %shard_map.94 = (bf16[1,1024,768]{2,1,0:T(8,128)(2,1)S(1)}, bf16[1,384,1024]{2,1,0:T(8,128)(2,1)S(1)}, bf16[48,1024]{1,0:T(8,128)(2,1)S(1)}, bf16[48,1024]{1,0:T...) custom-call(bf16[192,128]{1,0:T(8,128)(2,1)S(1)} %get-tuple-element.47.refs_0_.refs_4_, ...), custom_call_target="tpu_custom_call" | custom-call | flops 50331648 | bytes 5423616 | tf_op jit(solution)/shard_map/pallas_call | solution.py:27
  6.8 0.2 collective-permute-start.3
  7.0 1.9 %collective-permute-start.4 = (bf16[48,1024]{1,0:T(8,128)(2,1)S(1)}, bf16[48,1024]{1,0:T(8,128)(2,1)S(1)}, u32[]{:S(2)}, u32[]{:S(2)}) collective-permute-start(bf16[48,1024]{1,0:T(8,128)(2,1)S(1)} %get-tuple-element.52), channel_id=1, source_target_pairs={{0,2},{1,3},{2,0},{3,1},{4,6},{5,7},{6,4},{7,5},{8,10},{9,11},{10,... | collective-permute-start | bytes 294920 | tf_op jit(solution)/shard_map/ppermute | solution.py:228
  8.9 0.0 collective-permute-done.refs_1_
  8.9 0.0 collective-permute-start.5
  9.0 0.0 collective-permute-done.1.refs_2_
  9.0 1.3 %collective-permute-done.2.refs_3_ = bf16[48,1024]{1,0:T(8,128)(2,1)S(1)} collective-permute-done((bf16[48,1024]{1,0:T(8,128)(2,1)S(1)}, bf16[48,1024]{1,0:T(8,128)(2,1)S(1)}, u32[]{:S(2)}, u32[]{:S(2)}) %collective-permute-start.2) | collective-permute-done | bytes 98336 | tf_op jit(solution)/shard_map/ppermute | solution.py:228
  10.3 0.6 shard_map.95
  10.9 2.0 %collective-permute-done.4.refs_2_ = bf16[48,1024]{1,0:T(8,128)(2,1)S(1)} collective-permute-done((bf16[48,1024]{1,0:T(8,128)(2,1)S(1)}, bf16[48,1024]{1,0:T(8,128)(2,1)S(1)}, u32[]{:S(2)}, u32[]{:S(2)}) %collective-permute-start.4) | collective-permute-done | bytes 98336 | tf_op jit(solution)/shard_map/ppermute | solution.py:228
  12.9 1.6 %collective-permute-done.5.refs_3_ = bf16[48,1024]{1,0:T(8,128)(2,1)S(1)} collective-permute-done((bf16[48,1024]{1,0:T(8,128)(2,1)S(1)}, bf16[48,1024]{1,0:T(8,128)(2,1)S(1)}, u32[]{:S(2)}, u32[]{:S(2)}) %collective-permute-start.5) | collective-permute-done | bytes 98336 | tf_op jit(solution)/shard_map/ppermute | solution.py:228
  14.4 0.5 shard_map.96
  15.0 1.6 %collective-permute-start.9 = (bf16[192,512]{1,0:T(8,128)(2,1)S(1)}, bf16[192,512]{1,0:T(8,128)(2,1)S(1)}, u32[]{:S(2)}, u32[]{:S(2)}) collective-permute-start(bf16[192,512]{1,0:T(8,128)(2,1)S(1)} %get-tuple-element.67), channel_id=1, source_target_pairs={{0,4},{4,0},{8,12},{12,8},{16,20},{20,16},{24,28},{28,24},{1,5},{5... | collective-permute-start | bytes 589832 | tf_op jit(solution)/shard_map/ppermute | solution.py:228
  16.5 1.6 %collective-permute-start.13 = (bf16[192,512]{1,0:T(8,128)(2,1)S(1)}, bf16[192,512]{1,0:T(8,128)(2,1)S(1)}, u32[]{:S(2)}, u32[]{:S(2)}) collective-permute-start(bf16[192,512]{1,0:T(8,128)(2,1)S(1)} %get-tuple-element.72), channel_id=1, source_target_pairs={{0,8},{4,12},{8,0},{12,4},{16,24},{20,28},{24,16},{28,20},{1,9},{5... | collective-permute-start | bytes 589832 | tf_op jit(solution)/shard_map/ppermute | solution.py:228
  18.1 0.5 collective-permute-start.10
  18.6 0.5 collective-permute-start.19
  19.1 1.6 %collective-permute-start.16 = (bf16[192,256]{1,0:T(8,128)(2,1)S(1)}, bf16[192,256]{1,0:T(8,128)(2,1)S(1)}, u32[]{:S(2)}, u32[]{:S(2)}) collective-permute-start(bf16[192,256]{1,0:T(8,128)(2,1)S(1)} %get-tuple-element.57.d_gate.factor), channel_id=1, source_target_pairs={{0,8},{4,12},{8,0},{12,4},{16,24},{20,28},{24,16},{28,20},{1,9},{5... | collective-permute-start | bytes 294920 | tf_op jit(solution)/shard_map/ppermute | solution.py:228
  20.6 4.5 %collective-permute-done.10.factor_in = bf16[192,384]{1,0:T(8,128)(2,1)S(1)} collective-permute-done((bf16[192,384]{1,0:T(8,128)(2,1)S(1)}, bf16[192,384]{1,0:T(8,128)(2,1)S(1)}, u32[]{:S(2)}, u32[]{:S(2)}) %collective-permute-start.10) | collective-permute-done | bytes 147488 | tf_op jit(solution)/shard_map/ppermute | solution.py:228
  25.1 1.8 %collective-permute-start.14 = (bf16[192,128]{1,0:T(8,128)(2,1)S(1)}, bf16[192,128]{1,0:T(8,128)(2,1)S(1)}, u32[]{:S(2)}, u32[]{:S(2)}) collective-permute-start(bf16[192,128]{1,0:T(8,128)(2,1)S(1)} %get-tuple-element.56.d_first.factor), channel_id=1, source_target_pairs={{0,8},{4,12},{8,0},{12,4},{16,24},{20,28},{24,16},{28,20},{1,9},{5... | collective-permute-start | bytes 147464 | tf_op jit(solution)/shard_map/ppermute | solution.py:228
  26.9 0.0 collective-permute-done.9.rows_in
  26.9 0.5 shard_map.99
  27.4 0.3 collective-permute-start.11
  27.7 1.5 %collective-permute-done.16.factor_in = bf16[192,256]{1,0:T(8,128)(2,1)S(1)} collective-permute-done((bf16[192,256]{1,0:T(8,128)(2,1)S(1)}, bf16[192,256]{1,0:T(8,128)(2,1)S(1)}, u32[]{:S(2)}, u32[]{:S(2)}) %collective-permute-start.16) | collective-permute-done | bytes 98336 | tf_op jit(solution)/shard_map/ppermute | solution.py:228
  29.2 0.3 shard_map.102
  29.5 2.7 %collective-permute-start.17 = (bf16[256,256]{1,0:T(8,128)(2,1)S(1)}, bf16[256,256]{1,0:T(8,128)(2,1)S(1)}, u32[]{:S(2)}, u32[]{:S(2)}) collective-permute-start(bf16[256,256]{1,0:T(8,128)(2,1)S(1)} %get-tuple-element.76), channel_id=1, source_target_pairs={{0,16},{4,20},{8,24},{12,28},{16,0},{20,4},{24,8},{28,12},{1,17},{... | collective-permute-start | bytes 393224 | tf_op jit(solution)/shard_map/ppermute | solution.py:228
  32.2 0.5 shard_map.104
  32.7 0.3 collective-permute-start.20
  33.0 0.9 %shard_map.97 = (bf16[96,1024]{1,0:T(8,128)(2,1)S(1)}, bf16[96,1024]{1,0:T(8,128)(2,1)S(1)}, bf16[96,1024]{1,0:T(8,128)(2,1)S(1)}, bf16[96,1024]{1,0:T(8,128)(2,1)S(1)}) custom-call(bf16[192,384]{1,0:T(8,128)(2,1)S(1)} %get-tuple-element.49.act.factor, bf16[192,128]{1,0:T(8,128)(2,1)S(1)} %get-tuple-element.56.d_first.factor, ...), custom_call_target="tpu_custom_call" | custom-call | flops 452984832 | bytes 3588096 | tf_op jit(solution)/shard_map/pallas_call | solution.py:27
  33.9 0.0 copy-start
  33.9 0.0 copy-start.1
  33.9 0.1 collective-permute-start.6
  34.0 0.3 shard_map.101
  34.3 0.4 collective-permute-start.15
  34.7 6.8 %collective-permute-done.15.refs_1_.near_a = bf16[256,128]{1,0:T(8,128)(2,1)S(1)} collective-permute-done((bf16[256,128]{1,0:T(8,128)(2,1)S(1)}, bf16[256,128]{1,0:T(8,128)(2,1)S(1)}, u32[]{:S(2)}, u32[]{:S(2)}) %collective-permute-start.15) | collective-permute-done | bytes 65568 | tf_op jit(solution)/shard_map/ppermute | solution.py:228
  41.6 1.5 %collective-permute-start.7 = (bf16[96,1024]{1,0:T(8,128)(2,1)S(1)}, bf16[96,1024]{1,0:T(8,128)(2,1)S(1)}, u32[]{:S(2)}, u32[]{:S(2)}) collective-permute-start(bf16[96,1024]{1,0:T(8,128)(2,1)S(1)} %get-tuple-element.61), channel_id=1, source_target_pairs={{0,2},{1,3},{2,0},{3,1},{4,6},{5,7},{6,4},{7,5},{8,10},{9,11},{10,... | collective-permute-start | bytes 589832 | tf_op jit(solution)/shard_map/ppermute | solution.py:228
  43.1 0.1 collective-permute-start.18
  43.2 0.5 collective-permute-start.21
  43.8 2.6 %collective-permute-start.12 = (bf16[128,384]{1,0:T(8,128)(2,1)S(1)}, bf16[128,384]{1,0:T(8,128)(2,1)S(1)}, u32[]{:S(2)}, u32[]{:S(2)}) collective-permute-start(bf16[128,384]{1,0:T(8,128)(2,1)S(1)} %shard_map.100), channel_id=1, source_target_pairs={{0,16},{4,20},{8,24},{12,28},{16,0},{20,4},{24,8},{28,12},{1,17},{... | collective-permute-start | bytes 294920 | tf_op jit(solution)/shard_map/ppermute | solution.py:228
  46.3 3.0 %collective-permute-done.7.refs_2_ = bf16[96,1024]{1,0:T(8,128)(2,1)S(1)} collective-permute-done((bf16[96,1024]{1,0:T(8,128)(2,1)S(1)}, bf16[96,1024]{1,0:T(8,128)(2,1)S(1)}, u32[]{:S(2)}, u32[]{:S(2)}) %collective-permute-start.7) | collective-permute-done | bytes 196640 | tf_op jit(solution)/shard_map/ppermute | solution.py:228
  49.4 2.3 %collective-permute-done.8.refs_3_ = bf16[96,1024]{1,0:T(8,128)(2,1)S(1)} collective-permute-done((bf16[96,1024]{1,0:T(8,128)(2,1)S(1)}, bf16[96,1024]{1,0:T(8,128)(2,1)S(1)}, u32[]{:S(2)}, u32[]{:S(2)}) %collective-permute-start.8) | collective-permute-done | bytes 196640 | tf_op jit(solution)/shard_map/ppermute | solution.py:228
  51.7 1.1 %shard_map.98 = (bf16[128,1024]{1,0:T(8,128)(2,1)}, bf16[128,1024]{1,0:T(8,128)(2,1)}, f32[1,128]{1,0:T(1,128)}) custom-call(bf16[96,1024]{1,0:T(8,128)(2,1)S(1)} %get-tuple-element.59.refs_0_, bf16[96,1024]{1,0:T(8,128)(2,1)S(1)} %collective-permute-done.6.refs_1_, bf16[96,1024]{1,0:T(8,128)(2,1)S(1)} %collective-permute-done.7.refs_2_, ...), custom_call_target="tpu_custom_call" | custom-call | flops 100663296 | bytes 1623040 | tf_op jit(solution)/shard_map/pallas_call | solution.py:27
  52.8 1.3 %collective-permute-done.21.refs_2_ = bf16[128,384]{1,0:T(8,128)(2,1)S(1)} collective-permute-done((bf16[128,384]{1,0:T(8,128)(2,1)S(1)}, bf16[128,384]{1,0:T(8,128)(2,1)S(1)}, u32[]{:S(2)}, u32[]{:S(2)}) %collective-permute-start.21) | collective-permute-done | bytes 98336 | tf_op jit(solution)/shard_map/ppermute | solution.py:228
  54.1 0.8 %shard_map.106.out_in = f32[128,1152]{1,0:T(8,128)} custom-call(f32[128,128]{1,0:T(8,128)S(1)} %get-tuple-element.73.kept_a, bf16[256,128]{1,0:T(8,128)(2,1)S(1)} %collective-permute-done.15.refs_1_.near_a, f32[128,256]{1,0:T(8,128)S(1)} %get-tuple-element.75.kept_b, bf16[256,256]{1,0:T(8,128)(2,1)S(1)} %collective-permute-done.17.refs_3_.near_b, ...), custom_call_target="tpu_custom_call" | custom-call | bytes 1572864 | tf_op jit(solution)/shard_map/pallas_call | solution.py:27
  54.9 1.0 %collective-permute-done.12.distant = bf16[128,384]{1,0:T(8,128)(2,1)S(1)} collective-permute-done((bf16[128,384]{1,0:T(8,128)(2,1)S(1)}, bf16[128,384]{1,0:T(8,128)(2,1)S(1)}, u32[]{:S(2)}, u32[]{:S(2)}) %collective-permute-start.12) | collective-permute-done | bytes 98336 | tf_op jit(solution)/shard_map/ppermute | solution.py:228
  55.9 0.7 %shard_map.107 = f32[128,1152]{1,0:T(8,128)} custom-call(f32[128,384]{1,0:T(8,128)S(1)} %get-tuple-element.68.kept, bf16[256,384]{1,0:T(8,128)(2,1)S(1)} %collective-permute-done.11.refs_1_.near, bf16[128,384]{1,0:T(8,128)(2,1)S(1)} %collective-permute-done.12.distant, f32[128,1152]{1,0:T(8,128)} %shard_map.106.out_in), custom_call_target="tpu_custom_call", output_to_operand_aliasing={{}: (3, {})} | custom-call | bytes 1671168 | tf_op jit(solution)/shard_map/pallas_call | solution.py:27
  (15 shorter events, 0.1 us)
Async XLA Ops:
  1.9 7.1 %collective-permute-start = (bf16[48,1024]{1,0:T(8,128)(2,1)S(1)}, bf16[48,1024]{1,0:T(8,128)(2,1)S(1)}, u32[]{:S(2)}, u32[]{:S(2)}) collective-permute-start(bf16[48,1024]{1,0:T(8,128)(2,1)S(1)} %get-tuple-element.44), channel_id=1, source_target_pairs={{0,1},{1,0},{2,3},{3,2},{4,5},{5,4},{6,7},{7,6},{8,9},{9,8},{10,11... | collective-permute-start | bytes 294920 | tf_op jit(solution)/shard_map/ppermute | solution.py:228
  2.4 6.5 %collective-permute-start.1 = (bf16[48,1024]{1,0:T(8,128)(2,1)S(1)}, bf16[48,1024]{1,0:T(8,128)(2,1)S(1)}, u32[]{:S(2)}, u32[]{:S(2)}) collective-permute-start(bf16[48,1024]{1,0:T(8,128)(2,1)S(1)} %get-tuple-element.45), channel_id=1, source_target_pairs={{0,2},{1,3},{2,0},{3,1},{4,6},{5,7},{6,4},{7,5},{8,10},{9,11},{10,... | collective-permute-start | bytes 294920 | tf_op jit(solution)/shard_map/ppermute | solution.py:228
  5.0 5.3 %collective-permute-start.2 = (bf16[48,1024]{1,0:T(8,128)(2,1)S(1)}, bf16[48,1024]{1,0:T(8,128)(2,1)S(1)}, u32[]{:S(2)}, u32[]{:S(2)}) collective-permute-start(bf16[48,1024]{1,0:T(8,128)(2,1)S(1)} %get-tuple-element.46), channel_id=1, source_target_pairs={{0,3},{1,2},{2,1},{3,0},{4,7},{5,6},{6,5},{7,4},{8,11},{9,10},{10,... | collective-permute-start | bytes 294920 | tf_op jit(solution)/shard_map/ppermute | solution.py:228
  6.8 4.1 %collective-permute-start.3 = (bf16[48,1024]{1,0:T(8,128)(2,1)S(1)}, bf16[48,1024]{1,0:T(8,128)(2,1)S(1)}, u32[]{:S(2)}, u32[]{:S(2)}) collective-permute-start(bf16[48,1024]{1,0:T(8,128)(2,1)S(1)} %get-tuple-element.51), channel_id=1, source_target_pairs={{0,1},{1,0},{2,3},{3,2},{4,5},{5,4},{6,7},{7,6},{8,9},{9,8},{10,11... | collective-permute-start | bytes 294920 | tf_op jit(solution)/shard_map/ppermute | solution.py:228
  7.0 5.9 %collective-permute-start.4 = (bf16[48,1024]{1,0:T(8,128)(2,1)S(1)}, bf16[48,1024]{1,0:T(8,128)(2,1)S(1)}, u32[]{:S(2)}, u32[]{:S(2)}) collective-permute-start(bf16[48,1024]{1,0:T(8,128)(2,1)S(1)} %get-tuple-element.52), channel_id=1, source_target_pairs={{0,2},{1,3},{2,0},{3,1},{4,6},{5,7},{6,4},{7,5},{8,10},{9,11},{10,... | collective-permute-start | bytes 294920 | tf_op jit(solution)/shard_map/ppermute | solution.py:228
  8.9 5.5 %collective-permute-start.5 = (bf16[48,1024]{1,0:T(8,128)(2,1)S(1)}, bf16[48,1024]{1,0:T(8,128)(2,1)S(1)}, u32[]{:S(2)}, u32[]{:S(2)}) collective-permute-start(bf16[48,1024]{1,0:T(8,128)(2,1)S(1)} %get-tuple-element.53), channel_id=1, source_target_pairs={{0,3},{1,2},{2,1},{3,0},{4,7},{5,6},{6,5},{7,4},{8,11},{9,10},{10,... | collective-permute-start | bytes 294920 | tf_op jit(solution)/shard_map/ppermute | solution.py:228
  15.0 12.0 %collective-permute-start.9 = (bf16[192,512]{1,0:T(8,128)(2,1)S(1)}, bf16[192,512]{1,0:T(8,128)(2,1)S(1)}, u32[]{:S(2)}, u32[]{:S(2)}) collective-permute-start(bf16[192,512]{1,0:T(8,128)(2,1)S(1)} %get-tuple-element.67), channel_id=1, source_target_pairs={{0,4},{4,0},{8,12},{12,8},{16,20},{20,16},{24,28},{28,24},{1,5},{5... | collective-permute-start | bytes 589832 | tf_op jit(solution)/shard_map/ppermute | solution.py:228
  16.5 12.7 %collective-permute-start.13 = (bf16[192,512]{1,0:T(8,128)(2,1)S(1)}, bf16[192,512]{1,0:T(8,128)(2,1)S(1)}, u32[]{:S(2)}, u32[]{:S(2)}) collective-permute-start(bf16[192,512]{1,0:T(8,128)(2,1)S(1)} %get-tuple-element.72), channel_id=1, source_target_pairs={{0,8},{4,12},{8,0},{12,4},{16,24},{20,28},{24,16},{28,20},{1,9},{5... | collective-permute-start | bytes 589832 | tf_op jit(solution)/shard_map/ppermute | solution.py:228
  18.1 7.0 %collective-permute-start.10 = (bf16[192,384]{1,0:T(8,128)(2,1)S(1)}, bf16[192,384]{1,0:T(8,128)(2,1)S(1)}, u32[]{:S(2)}, u32[]{:S(2)}) collective-permute-start(bf16[192,384]{1,0:T(8,128)(2,1)S(1)} %get-tuple-element.49.act.factor), channel_id=1, source_target_pairs={{0,4},{4,0},{8,12},{12,8},{16,20},{20,16},{24,28},{28,24},{1,5},{5... | collective-permute-start | bytes 442376 | tf_op jit(solution)/shard_map/ppermute | solution.py:228
  18.6 13.6 %collective-permute-start.19 = (bf16[192,384]{1,0:T(8,128)(2,1)S(1)}, bf16[192,384]{1,0:T(8,128)(2,1)S(1)}, u32[]{:S(2)}, u32[]{:S(2)}) collective-permute-start(bf16[192,384]{1,0:T(8,128)(2,1)S(1)} %get-tuple-element.58.d_up.factor), channel_id=1, source_target_pairs={{0,8},{4,12},{8,0},{12,4},{16,24},{20,28},{24,16},{28,20},{1,9},{5... | collective-permute-start | bytes 442376 | tf_op jit(solution)/shard_map/ppermute | solution.py:228
  19.1 10.1 %collective-permute-start.16 = (bf16[192,256]{1,0:T(8,128)(2,1)S(1)}, bf16[192,256]{1,0:T(8,128)(2,1)S(1)}, u32[]{:S(2)}, u32[]{:S(2)}) collective-permute-start(bf16[192,256]{1,0:T(8,128)(2,1)S(1)} %get-tuple-element.57.d_gate.factor), channel_id=1, source_target_pairs={{0,8},{4,12},{8,0},{12,4},{16,24},{20,28},{24,16},{28,20},{1,9},{5... | collective-permute-start | bytes 294920 | tf_op jit(solution)/shard_map/ppermute | solution.py:228
  25.1 8.9 %collective-permute-start.14 = (bf16[192,128]{1,0:T(8,128)(2,1)S(1)}, bf16[192,128]{1,0:T(8,128)(2,1)S(1)}, u32[]{:S(2)}, u32[]{:S(2)}) collective-permute-start(bf16[192,128]{1,0:T(8,128)(2,1)S(1)} %get-tuple-element.56.d_first.factor), channel_id=1, source_target_pairs={{0,8},{4,12},{8,0},{12,4},{16,24},{20,28},{24,16},{28,20},{1,9},{5... | collective-permute-start | bytes 147464 | tf_op jit(solution)/shard_map/ppermute | solution.py:228
  27.4 15.8 %collective-permute-start.11 = (bf16[256,384]{1,0:T(8,128)(2,1)S(1)}, bf16[256,384]{1,0:T(8,128)(2,1)S(1)}, u32[]{:S(2)}, u32[]{:S(2)}) collective-permute-start(bf16[256,384]{1,0:T(8,128)(2,1)S(1)} %get-tuple-element.69), channel_id=1, source_target_pairs={{0,8},{4,12},{8,0},{12,4},{16,24},{20,28},{24,16},{28,20},{1,9},{5... | collective-permute-start | bytes 589832 | tf_op jit(solution)/shard_map/ppermute | solution.py:228
  29.5 13.5 %collective-permute-start.17 = (bf16[256,256]{1,0:T(8,128)(2,1)S(1)}, bf16[256,256]{1,0:T(8,128)(2,1)S(1)}, u32[]{:S(2)}, u32[]{:S(2)}) collective-permute-start(bf16[256,256]{1,0:T(8,128)(2,1)S(1)} %get-tuple-element.76), channel_id=1, source_target_pairs={{0,16},{4,20},{8,24},{12,28},{16,0},{20,4},{24,8},{28,12},{1,17},{... | collective-permute-start | bytes 393224 | tf_op jit(solution)/shard_map/ppermute | solution.py:228
  32.7 10.4 %collective-permute-start.20 = (bf16[256,384]{1,0:T(8,128)(2,1)S(1)}, bf16[256,384]{1,0:T(8,128)(2,1)S(1)}, u32[]{:S(2)}, u32[]{:S(2)}) collective-permute-start(bf16[256,384]{1,0:T(8,128)(2,1)S(1)} %get-tuple-element.80), channel_id=1, source_target_pairs={{0,4},{4,0},{8,12},{12,8},{16,20},{20,16},{24,28},{28,24},{1,5},{5... | collective-permute-start | bytes 589832 | tf_op jit(solution)/shard_map/ppermute | solution.py:228
  33.9 17.8 %copy-start = (bf16[128,1024]{1,0:T(8,128)(2,1)S(1)}, bf16[128,1024]{1,0:T(8,128)(2,1)}, u32[]{:S(2)}) copy-start(bf16[128,1024]{1,0:T(8,128)(2,1)} %refs_6_.1) | copy-start | bytes 786436
  33.9 17.8 %copy-start.1 = (f32[128,1]{0,1:T(1,128)S(1)}, f32[128,1]{0,1:T(1,128)}, u32[]{:S(2)}) copy-start(f32[128,1]{0,1:T(1,128)} %param.8) | copy-start | bytes 1540
  33.9 9.8 %collective-permute-start.6 = (bf16[96,1024]{1,0:T(8,128)(2,1)S(1)}, bf16[96,1024]{1,0:T(8,128)(2,1)S(1)}, u32[]{:S(2)}, u32[]{:S(2)}) collective-permute-start(bf16[96,1024]{1,0:T(8,128)(2,1)S(1)} %get-tuple-element.60), channel_id=1, source_target_pairs={{0,1},{1,0},{2,3},{3,2},{4,5},{5,4},{6,7},{7,6},{8,9},{9,8},{10,11... | collective-permute-start | bytes 589832 | tf_op jit(solution)/shard_map/ppermute | solution.py:228
  34.3 7.2 %collective-permute-start.15 = (bf16[256,128]{1,0:T(8,128)(2,1)S(1)}, bf16[256,128]{1,0:T(8,128)(2,1)S(1)}, u32[]{:S(2)}, u32[]{:S(2)}) collective-permute-start(bf16[256,128]{1,0:T(8,128)(2,1)S(1)} %get-tuple-element.74), channel_id=1, source_target_pairs={{0,16},{4,20},{8,24},{12,28},{16,0},{20,4},{24,8},{28,12},{1,17},{... | collective-permute-start | bytes 196616 | tf_op jit(solution)/shard_map/ppermute | solution.py:228
  41.6 7.8 %collective-permute-start.7 = (bf16[96,1024]{1,0:T(8,128)(2,1)S(1)}, bf16[96,1024]{1,0:T(8,128)(2,1)S(1)}, u32[]{:S(2)}, u32[]{:S(2)}) collective-permute-start(bf16[96,1024]{1,0:T(8,128)(2,1)S(1)} %get-tuple-element.61), channel_id=1, source_target_pairs={{0,2},{1,3},{2,0},{3,1},{4,6},{5,7},{6,4},{7,5},{8,10},{9,11},{10,... | collective-permute-start | bytes 589832 | tf_op jit(solution)/shard_map/ppermute | solution.py:228
  43.1 8.6 %collective-permute-start.8 = (bf16[96,1024]{1,0:T(8,128)(2,1)S(1)}, bf16[96,1024]{1,0:T(8,128)(2,1)S(1)}, u32[]{:S(2)}, u32[]{:S(2)}) collective-permute-start(bf16[96,1024]{1,0:T(8,128)(2,1)S(1)} %get-tuple-element.62), channel_id=1, source_target_pairs={{0,3},{1,2},{2,1},{3,0},{4,7},{5,6},{6,5},{7,4},{8,11},{9,10},{10,... | collective-permute-start | bytes 589832 | tf_op jit(solution)/shard_map/ppermute | solution.py:228
  43.1 9.7 %collective-permute-start.18 = (bf16[128,384]{1,0:T(8,128)(2,1)S(1)}, bf16[128,384]{1,0:T(8,128)(2,1)S(1)}, u32[]{:S(2)}, u32[]{:S(2)}) collective-permute-start(bf16[128,384]{1,0:T(8,128)(2,1)S(1)} %shard_map.103), channel_id=1, source_target_pairs={{0,4},{4,0},{8,12},{12,8},{16,20},{20,16},{24,28},{28,24},{1,5},{5... | collective-permute-start | bytes 294920 | tf_op jit(solution)/shard_map/ppermute | solution.py:228
  43.2 10.8 %collective-permute-start.21 = (bf16[128,384]{1,0:T(8,128)(2,1)S(1)}, bf16[128,384]{1,0:T(8,128)(2,1)S(1)}, u32[]{:S(2)}, u32[]{:S(2)}) collective-permute-start(bf16[128,384]{1,0:T(8,128)(2,1)S(1)} %shard_map.105), channel_id=1, source_target_pairs={{0,16},{4,20},{8,24},{12,28},{16,0},{20,4},{24,8},{28,12},{1,17},{... | collective-permute-start | bytes 294920 | tf_op jit(solution)/shard_map/ppermute | solution.py:228
  43.8 12.1 %collective-permute-start.12 = (bf16[128,384]{1,0:T(8,128)(2,1)S(1)}, bf16[128,384]{1,0:T(8,128)(2,1)S(1)}, u32[]{:S(2)}, u32[]{:S(2)}) collective-permute-start(bf16[128,384]{1,0:T(8,128)(2,1)S(1)} %shard_map.100), channel_id=1, source_target_pairs={{0,16},{4,20},{8,24},{12,28},{16,0},{20,4},{24,8},{28,12},{1,17},{... | collective-permute-start | bytes 294920 | tf_op jit(solution)/shard_map/ppermute | solution.py:228
